TPU v7x, 32 devices: a whole 2x2x4 slice. The times are simulated.
32 devices in a mesh: groups: 2 (over y), cells: 4 (over z), corners: 2 (over x), kern: 2 (over core).
Axes of the slice: x: 2, y: 2, z: 4, core: 2. Of those that a mesh axis runs over, the one named last changes fastest.
Arguments:
- theta: float32 [64, 128, 128], P(('groups', 'cells')), parts along dimension 0, may hold values from -8 to 8
- target: bfloat16 [16, 128, 128], P(('groups', 'cells')), parts along dimension 0, may hold values from 0 to 1
- kernels: float32 [2, 2, 24, 35, 35], P(None, 'corners', 'kern'), may hold values from -25.33743 to 25.33743
- dose: float32 [2], P('corners'), may hold values from 0.6 to 1
- inst_owner: int32 [128, 1], P(('groups', 'cells')), parts along dimension 0, may hold values from 0 to 3; in each aligned block of 16 rows (0 to 15, 16 to 31, ...) at most 8 rows name the same one
- inst_local: int32 [128], P(('groups', 'cells')), parts along dimension 0, may hold values from 0 to 7
- inst_shift: int32 [128], P(('groups', 'cells')), parts along dimension 0, may hold values from 0 to 127
Outputs:
- theta_out: float32 [64, 128, 128], P(('groups', 'cells'), ('corners', 'kern')), parts along dimension 0
There are 2 independent parts, one for each index of `groups`. A program takes and returns all parts, laid end to end along the dimension named above; an argument that names none is the same for every part. Nothing has to cross between parts.
Inputs may be any that keep to these rules, and one draw needn't show every extreme that they name: `inst_owner`: within the rows of one device (aligned blocks of 16 rows) no owner is named by more than 8 rows, and in some block one owner is named by exactly 8.
All inputs are finite; a program needn't handle non-finite values.
Results may differ from a plain program's by a relative error of at most 0.003.
Values may be sent and summed in bfloat16 or wider, within the bound.
No kernel may reach another device: no remote copies, remote signals or barrier semaphores. Data moves between devices by JAX's collectives and lax.ppermute only.
A program may use at most 64 MiB of HBM per device.

v0:
```python
import functools

import jax
import jax.numpy as jnp
import numpy as np
from jax import lax
from jax.experimental import pallas as pl
from jax.experimental.pallas import tpu as pltpu
from jax.sharding import PartitionSpec as P


ITERS = 2
LR = 0.25
EPS = 1e-06
STEEP = 3.0
LANES = 128
HALF = LANES // 2
INFO = 16
CHUNK = 8
BF = jnp.bfloat16
F32 = jnp.float32


def up(value, step):
    return -(-value // step) * step


def split(array):
    high = np.asarray(array, np.float32).astype(BF)
    low = (np.asarray(array, np.float32) - high.astype(np.float32)).astype(BF)
    return high, low


class Tables:
    def __init__(self, cell, freq):
        self.cell, self.freq = cell, freq
        self.mid = freq // 2
        self.rows = up(self.mid + 1, 8)
        self.grid = min(cell, up(4 * self.mid + 1, 8))
        rows, grid, mid = self.rows, self.grid, self.mid
        turn = 2.0 * np.pi / cell
        f = np.arange(mid + 1)
        g = np.arange(freq) - mid
        pixels = np.arange(cell)
        fy = np.zeros((cell, LANES))
        phase = (pixels[:, None] * g[None, :] % cell) * turn
        fy[:, :freq] = np.cos(phase)
        fy[:, HALF : HALF + freq] = -np.sin(phase)
        self.fy = np.concatenate(split(fy), axis=1)
        fx = np.zeros((2 * rows, cell))
        phase = (f[:, None] * pixels[None, :] % cell) * turn
        fx[: mid + 1] = np.cos(phase)
        fx[rows : rows + mid + 1] = np.sin(phase)
        self.fx = np.concatenate(split(fx), axis=0)
        ex = np.concatenate([fx[:rows].T, -fx[rows:].T], axis=1)
        self.ex = ex.astype(np.float32).astype(BF)
        gy = np.zeros((LANES, 2 * cell))
        phase = (g[:, None] * pixels[None, :] % cell) * turn
        gy[:freq, :cell] = np.cos(phase)
        gy[:freq, cell:] = np.sin(phase)
        gy[HALF : HALF + freq, :cell] = -np.sin(phase)
        gy[HALF : HALF + freq, cell:] = np.cos(phase)
        self.gy = gy.astype(np.float32).astype(BF)
        both = np.concatenate([gy, np.roll(gy, HALF, axis=0)], axis=0)
        self.gyy = both.astype(np.float32).astype(BF)
        self.gyy_t = self.gyy.T.copy()
        gx = np.zeros((2 * grid, 4 * rows))
        phase = (f[None, :] * np.arange(grid)[:, None] % grid) * (2.0 * np.pi / grid)
        cos, sin = np.zeros((grid, rows)), np.zeros((grid, rows))
        cos[:, : mid + 1], sin[:, : mid + 1] = np.cos(phase), np.sin(phase)
        gx[:grid] = np.concatenate([cos, cos, -sin, -sin], axis=1)
        gx[grid:] = np.concatenate([sin, -sin, cos, -cos], axis=1)
        self.gx = gx.astype(np.float32).astype(BF)
        self.gx_t = self.gx.T.copy()
        u = np.arange(-2 * mid, 2 * mid + 1)
        if grid == cell:
            weights = np.eye(cell)
        else:
            diff = pixels[:, None] / cell - np.arange(grid)[None, :] / grid
            weights = np.cos(2.0 * np.pi * diff[:, :, None] * u).sum(-1) / grid
        high, low = split(weights)
        self.w = np.zeros((cell, up(3 * grid, 16)), np.float32).astype(BF)
        self.w[:, : 3 * grid] = np.concatenate([high, high, low], axis=1)
        self.w_t = high.T.copy()
        ph = np.zeros((cell, 2 * LANES))
        phase = (pixels[:, None] * g[None, :] % cell) * turn
        ph[:, :freq] = ph[:, HALF : HALF + freq] = np.cos(phase)
        ph[:, LANES : LANES + freq] = np.sin(phase)
        ph[:, LANES + HALF : LANES + HALF + freq] = -np.sin(phase)
        self.ph = ph.astype(np.float32)
        self.ph_split = np.concatenate(split(ph), axis=1)


def packing(tabs):
    sent = tabs.rows - 8
    free = HALF - tabs.freq
    extra = tabs.mid + 1 - sent
    pieces = -(-tabs.freq // free) if free > 0 else 0
    if sent % 16 or free < 8 or extra < 1 or extra * pieces > 8:
        return up(tabs.rows, 16), []
    steps = []
    for p in range(pieces):
        begin = p * free
        steps.append((begin, min(free, tabs.freq - begin), p * extra, extra))
    return sent, steps


def inside(first, count, value):
    return (value >= first) & (value < first + count)


def pack(tabs, spec):
    sent, steps = packing(tabs)
    if not steps:
        return jnp.concatenate([spec, jnp.zeros((sent - tabs.rows, LANES), F32)], axis=0).astype(BF)
    row = lax.broadcasted_iota(jnp.int32, (8, LANES), 0)
    col = lane_of((8, LANES)) % HALF
    top, rest = spec[:8], spec[sent:]
    for begin, width, where, extra in steps:
        moved = pltpu.roll(rest, tabs.freq - begin, 1)
        if where:
            moved = pltpu.roll(moved, where, 0)
        here = inside(where, extra, row) & inside(tabs.freq, width, col)
        top = jnp.where(here, moved, top)
    return jnp.concatenate([top, spec[8:sent]], axis=0).astype(BF)


def unpack(tabs, sent_spec):
    _, steps = packing(tabs)
    if not steps:
        return sent_spec[: tabs.rows].astype(F32)
    spec = sent_spec.astype(F32)
    row = lax.broadcasted_iota(jnp.int32, (8, LANES), 0)
    col = lane_of((8, LANES)) % HALF
    rest = jnp.zeros((8, LANES), F32)
    for begin, width, where, extra in steps:
        moved = pltpu.roll(spec[:8], LANES - (tabs.freq - begin), 1)
        if where:
            moved = pltpu.roll(moved, 8 - where, 0)
        here = inside(0, extra, row) & inside(begin, width, col)
        rest = jnp.where(here, moved, rest)
    return jnp.concatenate([spec, rest], axis=0)


def dot(a, b, **kw):
    return jnp.dot(a, b, preferred_element_type=F32, **kw)


def swap(x):
    return pltpu.roll(x, HALF, 1)


def lane_of(shape):
    return lax.broadcasted_iota(jnp.int32, shape, len(shape) - 1)


def arrange_body(tabs, kern, out):
    freq, mid, rows = tabs.freq, tabs.mid, tabs.rows
    number, tall = out.shape[0], up(freq, 8)
    side = jnp.zeros((freq, HALF - freq), F32)
    below = jnp.zeros((tall - freq, LANES), F32)
    rights = []
    for k in range(number):
        both = jnp.concatenate([kern[0, 0, k], side, kern[1, 0, k], side], axis=1)
        rights.append(jnp.concatenate([both, below], axis=0))
    rights = jnp.concatenate(rights, axis=0).astype(BF)
    row = lax.broadcasted_iota(jnp.int32, (LANES, LANES), 0)
    col = lane_of((LANES, LANES))
    same = (row // HALF == col // HALF) & (row % HALF + col % HALF == freq - 1)
    turned = jnp.where(same, jnp.where(row < HALF, 1.0, -1.0), 0.0).astype(BF)
    lefts = dot(rights, turned)
    rights = rights.astype(F32)
    row = lax.broadcasted_iota(jnp.int32, (2 * rows, 2 * tall), 0)
    col = lane_of((2 * rows, 2 * tall))
    upper = (row <= mid) & (col == mid + row)
    lower = (row > rows) & (row <= rows + mid) & (col == tall + mid - (row - rows))
    pick = jnp.where(upper | lower, 1.0, 0.0).astype(BF)
    for k in range(0, number, 2):
        columns = [
            jnp.concatenate(
                [rights[m * tall : (m + 1) * tall], lefts[m * tall : (m + 1) * tall]], axis=0
            )
            for m in range(k, min(k + 2, number))
        ]
        res = dot(pick, jnp.concatenate(columns, axis=1).astype(BF)).astype(BF)
        for p in range(len(columns)):
            out[k + p] = res[:, p * LANES : (p + 1) * LANES]


def spectra(tabs, slots, theta, fy, fx):
    cells, cell, rows = theta.shape[0], tabs.cell, tabs.rows
    mask = jax.nn.sigmoid(theta).astype(BF).reshape(cells * cell, cell)
    along = dot(mask, fy[...])
    along = along[:, :LANES] + along[:, LANES:]
    sign = jnp.where(lane_of((rows, LANES)) < HALF, 1.0, -1.0)
    row_at = lax.broadcasted_iota(jnp.int32, (rows, LANES), 0)
    centre = jnp.where((row_at == 0) & (lane_of((rows, LANES)) == tabs.mid), 1.0 / slots, 0.0)
    scale = 2.0 / (slots * cell * cell)
    specs = []
    for c in range(cells):
        part = along[c * cell : (c + 1) * cell]
        high = part.astype(BF)
        low = (part - high.astype(F32)).astype(BF)
        res = dot(fx[...], jnp.concatenate([high, low], axis=1))
        res = res[: 2 * rows, :LANES] + res[: 2 * rows, LANES:] + res[2 * rows :, :LANES]
        spec = res[:rows] + swap(res[rows:]) * sign
        specs.append(spec * scale - centre)
    return specs


def first_body(tabs, slots, owner, local, shift, theta, fy, fx, out, table):
    sent = packing(tabs)[0]
    for c, spec in enumerate(spectra(tabs, slots, theta[...], fy, fx)):
        out[c * sent : (c + 1) * sent] = pack(tabs, spec)
    base = theta.shape[0] * sent
    row = lax.broadcasted_iota(jnp.int32, (INFO, LANES), 0)
    col = lane_of((INFO, LANES))
    info = jnp.zeros((INFO, LANES), jnp.int32)
    for i in range(local.shape[0]):
        table[0, i] = owner[i]
        table[1, i] = local[i]
        table[2, i] = shift[i]
        value = jnp.where(row == 0, owner[i], jnp.where(row == 1, local[i], shift[i]))
        info = jnp.where((col == i) & (row < 3), value, info)
    out[base : base + INFO] = info.astype(F32).astype(BF)


def counts(tabs, n, tiles, cells, slots, ph, payload, out):
    z = lax.axis_index("cells")
    base = cells * packing(tabs)[0]
    row = lax.broadcasted_iota(jnp.int32, (tiles * cells, LANES), 0)
    col = lane_of((tiles * cells, LANES))
    shift_at = lax.broadcasted_iota(jnp.int32, (tabs.cell, LANES), 0)
    numbers = []
    for k in range(n):
        info = payload[k][base : base + INFO].astype(F32).astype(jnp.int32)
        owner, local, shift = info[0:1], info[1:2], info[2:3]
        mine = (owner == z) & (local == row % cells) & (col // slots == row // cells)
        mine = mine & (col < tiles * slots)
        chosen = jnp.where(mine, 1.0, 0.0).astype(BF)
        hot = jnp.where(shift == shift_at, 1.0, 0.0).astype(BF)
        numbers.append(
            lax.dot_general(chosen, hot, (((1,), (1,)), ((), ())), preferred_element_type=F32)
        )
    sums = dot(jnp.concatenate(numbers, axis=0).astype(BF), ph[...])
    sums = sums[:, : 2 * LANES] + sums[:, 2 * LANES :]
    for k in range(n):
        place = source(n, z, k)
        part = sums[k * tiles * cells : (k + 1) * tiles * cells]
        out[pl.ds(place * tiles, tiles)] = part.reshape(tiles, cells, 2 * LANES)


def tile_body(tabs, n, cells, tiles, copies, table, dose, *refs):
    payload, (ph, *rest, out, held, wide, tall, near) = refs[:n], refs[n:]
    slots = table.shape[1] // tiles
    z, j = lax.axis_index("cells"), lax.axis_index("kern")
    sent = packing(tabs)[0]
    for k in range(n):
        held[pl.ds(k * cells, cells)] = payload[k][0 : cells * sent].reshape(cells, sent, LANES)
    spec = jnp.zeros((tabs.rows, LANES), F32)
    for s in range(slots):
        i = j * slots + s
        which = source(n, z, table[0, i]) * cells + table[1, i]
        one = unpack(tabs, held[which])
        turn = ph[pl.ds(table[2, i], 1)]
        spec = spec + one * turn[:, :LANES] + swap(one) * turn[:, LANES:]
    tile_gradient(tabs, tiles, copies, spec, dose, rest, out, wide, tall, near)


def again_body(tabs, n, tiles, copies, dose, *refs):
    parts, (*rest, out, wide, tall, near) = refs[:n], refs[n:]
    total = parts[0][...].astype(F32)
    for k in range(1, n):
        total = total + parts[k][...].astype(F32)
    spec = unpack(tabs, total)
    tile_gradient(tabs, tiles, copies, spec, dose, rest, out, wide, tall, near)


def tile_gradient(tabs, tiles, copies, spec, dose, rest, out, wide, tall, near):
    arranged, (target, gyy, gyy_t, gx, gx_t, w, w_t) = rest[:tiles], rest[tiles:]
    rows, cell, grid = tabs.rows, tabs.cell, tabs.grid
    left = lane_of((rows, LANES)) < HALF
    other = swap(spec)
    real = jnp.where(left, spec, other)
    imag = jnp.where(left, other, -spec)
    real = jnp.concatenate([real, real], axis=0)
    imag = jnp.concatenate([imag, imag], axis=0)
    wanted = target[lax.axis_index("kern")].astype(F32)
    span = 2 * rows
    members = [(ref, k) for ref in arranged for k in range(ref.shape[0])]
    number = len(members)
    for m, (ref, k) in enumerate(members):
        kern = ref[k].astype(F32)
        wide[m * span : (m + 1) * span, :LANES] = (kern * real).astype(BF)
        wide[m * span : (m + 1) * span, LANES:] = (kern * imag).astype(BF)
    for first in range(0, number, CHUNK):
        last = min(first + CHUNK, number)
        res = dot(wide[first * span : last * span], gyy[...])
        for m in range(first, last):
            part = res[(m - first) * span : (m - first + 1) * span]
            tall[m] = jnp.concatenate([part[:, :cell], part[:, cell:]], axis=0).astype(BF)
    total = jnp.zeros((grid, cell), F32)
    for m in range(0, number, 2):
        pair = [tall[m + p] for p in range(min(2, number - m))]
        fields = dot(gx[...], jnp.concatenate(pair, axis=1))
        for p in range(len(pair)):
            one = fields[:, p * cell : (p + 1) * cell]
            near[m + p] = one
            total = total + (one[:grid] * one[:grid] + one[grid:] * one[grid:])
    high = total.astype(BF).astype(F32)
    stack = [high, total - high, high]
    if w.shape[1] > 3 * grid:
        stack.append(jnp.zeros((w.shape[1] - 3 * grid, cell), F32))
    image = dot(w[...], jnp.concatenate(stack, axis=0).astype(BF))
    resist = jax.nn.sigmoid(STEEP * (dose[0] * image - 1.0))
    pressure = 4.0 * STEEP * dose[0] * (resist - wanted) * resist * (1.0 - resist)
    push = dot(w_t[...], pressure.astype(BF))
    for m in range(0, number, 2):
        pair = []
        for p in range(min(2, number - m)):
            one = near[m + p]
            pair.append(jnp.concatenate([one[:grid] * push, one[grid:] * push], axis=0))
        back = dot(gx_t[...], jnp.concatenate(pair, axis=1).astype(BF)).astype(BF)
        for p in range(len(pair)):
            at_row = (m + p) * span
            wide[at_row : at_row + span, :LANES] = back[:span, p * cell : (p + 1) * cell]
            wide[at_row : at_row + span, LANES:] = back[span:, p * cell : (p + 1) * cell]
    sum_real = jnp.zeros((span, LANES), F32)
    sum_imag = jnp.zeros((span, LANES), F32)
    for first in range(0, number, CHUNK):
        last = min(first + CHUNK, number)
        res = dot(wide[first * span : last * span], gyy_t[...])
        for m in range(first, last):
            ref, k = members[m]
            kern = ref[k].astype(F32)
            part = res[(m - first) * span : (m - first + 1) * span]
            sum_real = sum_real + kern * part[:, :LANES]
            sum_imag = sum_imag + kern * part[:, LANES:]
    sum_real = sum_real[:rows] + sum_real[rows:]
    sum_imag = sum_imag[:rows] + sum_imag[rows:]
    grad = jnp.where(left, sum_real + swap(sum_real), swap(sum_imag - swap(sum_imag)))
    grad = pack(tabs, grad)
    for copy in range(copies):
        out[copy] = grad


def gradients(tabs, slots, corners, kern, theta, grads, sums, gy, ex):
    tiles, cells = sums.shape[0], theta.shape[0]
    rows, cell = tabs.rows, tabs.cell
    pieces = []
    own = []
    for t in range(tiles):
        z, j = t // kern, t % kern
        parts = [grads[(z * corners + x) * kern + j].astype(F32) for x in range(corners)]
        own.append(unpack(tabs, sum(parts[1:], parts[0])))
    swapped = [swap(grad) for grad in own]
    for c in range(cells):
        total = jnp.zeros((rows, LANES), F32)
        for t in range(tiles):
            turn = sums[t, c : c + 1]
            total = total + own[t] * turn[:, :LANES] - swapped[t] * turn[:, LANES:]
        pieces.append(total * (2.0 / (slots * cell * cell)))
    rowed = dot(jnp.concatenate(pieces, axis=0).astype(BF), gy[...])
    result = []
    for first in range(0, cells, 2):
        columns = []
        for c in range(first, min(first + 2, cells)):
            part = rowed[c * rows : (c + 1) * rows]
            columns.append(jnp.concatenate([part[:, :cell], part[:, cell:]], axis=0))
        planes = dot(ex[...], jnp.concatenate(columns, axis=1).astype(BF))
        for p in range(len(columns)):
            squash = jax.nn.sigmoid(theta[first + p])
            gradient = planes[:, p * cell : (p + 1) * cell] * squash * (1.0 - squash)
            power = jnp.sum(gradient * gradient, axis=0, keepdims=True)
            power = jnp.sum(power, axis=1, keepdims=True)
            result.append((gradient, LR * lax.rsqrt(power / (cell * cell) + EPS)))
    return result


def update_body(tabs, slots, corners, kern, n, theta, grads, ph, gy, ex, fy, fx, *refs):
    heard, (out, sums, *parts) = refs[:n], refs[n:]
    counts(tabs, n, kern, theta.shape[0], slots, ph, heard, sums)
    for c, (gradient, rate) in enumerate(
        gradients(tabs, slots, corners, kern, theta, grads, sums, gy, ex)
    ):
        out[c] = theta[c] - rate * gradient
    specs = spectra(tabs, slots, out[...], fy, fx)
    swapped = [swap(spec) for spec in specs]
    z, j = lax.axis_index("cells"), lax.axis_index("kern")
    for k in range(n):
        turns = sums[target_of(n, z, k) * kern + j]
        total = jnp.zeros((tabs.rows, LANES), F32)
        for c, spec in enumerate(specs):
            turn = turns[c : c + 1]
            total = total + spec * turn[:, :LANES] + swapped[c] * turn[:, LANES:]
        parts[k][...] = pack(tabs, total)


def last_body(tabs, slots, corners, kern, theta, grads, sums, gy, ex, out, held, ready, sem):
    band = out.shape[1]
    start = pl.multiple_of(lax.axis_index(("corners", "kern")) * band, band)
    copies = []
    for c, (gradient, rate) in enumerate(
        gradients(tabs, slots, corners, kern, theta, grads, sums, gy, ex)
    ):
        held[c] = rate * gradient
        ready[c] = theta[c, pl.ds(start, band)] - held[c, pl.ds(start, band)]
        copies.append(pltpu.make_async_copy(ready.at[c], out.at[c], sem.at[c]))
        copies[-1].start()
    for copy in copies:
        copy.wait()


VMEM = pl.BlockSpec(memory_space=pltpu.VMEM)
SMEM = pl.BlockSpec(memory_space=pltpu.SMEM)


def call(body, scalars, arrays, outs, scratch=(), name=None, far=(), out_far=False):
    many = isinstance(outs, list)
    if name in ("tile", "again"):
        scalars = [pltpu.with_memory_space_constraint(array, pltpu.SMEM) for array in scalars]
    arrays = [
        array if place in far else pltpu.with_memory_space_constraint(array, pltpu.VMEM)
        for place, array in enumerate(arrays)
    ]
    out_spec = pl.BlockSpec(memory_space=pl.ANY) if out_far else VMEM
    return pl.pallas_call(
        body,
        out_shape=outs,
        in_specs=[SMEM] * len(scalars) + [VMEM] * len(arrays),
        out_specs=[
            SMEM if out.memory_space == pltpu.SMEM else VMEM for out in outs
        ] if many else out_spec,
        scratch_shapes=list(scratch),
    )(*scalars, *arrays)


def shape(dims, dtype):
    return pltpu.VMEM(dims, dtype)


def paired(n):
    return n & (n - 1) == 0


def source(n, z, step):
    return z ^ step if paired(n) else lax.rem(z - step + n, n)


def target_of(n, z, step):
    return z ^ step if paired(n) else lax.rem(z + step, n)


def shifted(array, axis, step):
    n = lax.axis_size(axis)
    moves = [(i, i ^ step if paired(n) else (i + step) % n) for i in range(n)]
    return lax.ppermute(array, axis, moves)


def per_device(theta, target, kernels, dose, inst_owner, inst_local, inst_shift):
    n = lax.axis_size("cells")
    n_kern = lax.axis_size("kern")
    n_corners = lax.axis_size("corners")
    cells, cell = theta.shape[0], theta.shape[1]
    tiles = target.shape[0]
    slots = inst_local.shape[0] // tiles
    assert tiles == n_kern
    tabs = Tables(cell, kernels.shape[3])
    inst_owner = inst_owner[:, 0]
    rows, sent = tabs.rows, packing(tabs)[0]
    band = cell // (n_kern * n_corners)
    payload, table = call(
        functools.partial(first_body, tabs, slots),
        [inst_owner, inst_local, inst_shift],
        [theta, tabs.fy, tabs.fx],
        [
            shape((cells * sent + INFO, LANES), BF),
            pltpu.SMEM((3, inst_local.shape[0]), jnp.int32),
        ],
        name="first",
        far=(0, 1, 2),
    )
    payloads = [payload]
    for k in range(1, n):
        payloads.append(shifted(payload, "cells", k))
    own = call(
        functools.partial(arrange_body, tabs),
        [],
        [kernels],
        shape((kernels.shape[2], 2 * rows, LANES), BF),
        name="arrange",
    )
    arranged = [own]
    for k in range(1, n_kern):
        arranged.append(shifted(own, "kern", k))
    copies = n * n_corners * n_kern
    count = n_kern * kernels.shape[2]
    scratch = [
        pltpu.VMEM((count * 2 * rows, 2 * LANES), BF),
        pltpu.VMEM((count, 4 * rows, cell), BF),
        pltpu.VMEM((count, 2 * tabs.grid, cell), F32),
    ]
    common = arranged + [target, tabs.gyy, tabs.gyy_t, tabs.gx, tabs.gx_t, tabs.w, tabs.w_t]
    everyone = ("cells", "corners", "kern")
    grads = call(
        functools.partial(tile_body, tabs, n, cells, tiles, copies),
        [table, dose],
        payloads + [tabs.ph] + common,
        shape((copies, sent, LANES), BF),
        scratch=[pltpu.VMEM((n * cells, sent, LANES), BF)] + scratch,
        name="tile",
    )
    for _ in range(1, ITERS):
        grads = lax.all_to_all(grads, everyone, 0, 0, tiled=True)
        theta, sums, *parts = call(
            functools.partial(update_body, tabs, slots, n_corners, n_kern, n),
            [],
            [theta, grads, tabs.ph_split, tabs.gy, tabs.ex, tabs.fy, tabs.fx] + payloads,
            [shape(theta.shape, F32), shape((n * tiles, cells, 2 * LANES), F32)]
            + [shape((sent, LANES), BF)] * n,
            name="update",
        )
        for k in range(1, n):
            parts[k] = shifted(parts[k], "cells", k)
        grads = call(
            functools.partial(again_body, tabs, n, tiles, copies),
            [dose],
            parts + common,
            shape((copies, sent, LANES), BF),
            scratch=scratch,
            name="again",
        )
    grads = lax.all_to_all(grads, everyone, 0, 0, tiled=True)
    return call(
        functools.partial(last_body, tabs, slots, n_corners, n_kern),
        [],
        [theta, grads, sums, tabs.gy, tabs.ex],
        jax.ShapeDtypeStruct((cells, band, cell), F32),
        scratch=[
            pltpu.VMEM((cells, cell, cell), F32),
            pltpu.VMEM((cells, band, cell), F32),
            pltpu.SemaphoreType.DMA((cells,)),
        ],
        name="last",
        out_far=True,
    )


def solution(mesh):
    in_specs = (
        P(("groups", "cells"), None, None),
        P(("groups", "cells"), None, None),
        P(None, "corners", "kern", None, None),
        P("corners"),
        P(("groups", "cells"), None),
        P(("groups", "cells")),
        P(("groups", "cells")),
    )
    out_specs = P(("groups", "cells"), ("corners", "kern"), None)
    return jax.shard_map(
        per_device, mesh=mesh, in_specs=in_specs, out_specs=out_specs, check_vma=False
    )
```

profile of v0, /device:TPU:0, one launch (start us, length us, event | category | flops | bytes accessed | tf_op | source)
XLA Modules:
  0.0 49.5 jit_solution(2919775734229332617)
XLA Ops:
  0.0 1.0 %copy.20.kern = f32[2,1,12,35,35]{4,3,2,1,0:T(8,128)S(1)} copy(f32[2,1,12,35,35]{4,1,3,2,0:T(1,128)} %param.21) | data formatting | bytes 235200 | tf_op args[2]
  1.0 0.0 copy-start.13
  1.1 0.4 shard_map.182.refs_5_.refs_4_
  1.4 0.6 %collective-permute-start.3 = (bf16[12,48,128]{2,1,0:T(8,128)(2,1)S(1)}, bf16[12,48,128]{2,1,0:T(8,128)(2,1)S(1)}, u32[]{:S(2)}, u32[]{:S(2)}) collective-permute-start(bf16[12,48,128]{2,1,0:T(8,128)(2,1)S(1)} %shard_map.182.refs_5_.refs_4_), channel_id=1, source_target_pairs={{0,1},{1,0},{2,3},{3,2},{4,5},{5,4},{6,7},{7,6},{8,9},{9,8},{10,11... | collective-permute-start | bytes 442376 | tf_op jit(solution)/shard_map/ppermute | solution.py:457
  2.0 0.0 copy-start.7
  2.0 0.0 copy-start.8
  2.0 0.0 copy-start.11
  2.1 1.9 %shard_map.181 = (bf16[144,128]{1,0:T(8,128)(2,1)S(1)}, s32[3,16]{1,0:T(4,128)S(4)}) custom-call(s32[16]{0:T(128)} %bitcast.1, s32[16]{0:T(128)} %local.1, s32[16]{0:T(128)} %shift.1, f32[8,128,128]{2,1,0:T(8,128)} %theta.3, bf16[128,256]{1,0:T(8,128)(2,1)} %constant.24.clone.fy, bf16[96,128]{1,0:T(8,128)(2,1)} %constant.25.clone.fx), custom_call_target="tpu_custom_call" | custom-call | tf_op jit(solution)/shard_map/pallas_call | solution.py:427
  3.9 4.7 %collective-permute-start.2 = (bf16[144,128]{1,0:T(8,128)(2,1)S(1)}, bf16[144,128]{1,0:T(8,128)(2,1)S(1)}, u32[]{:S(2)}, u32[]{:S(2)}) collective-permute-start(bf16[144,128]{1,0:T(8,128)(2,1)S(1)} %get-tuple-element.14.refs_0_), channel_id=1, source_target_pairs={{0,12},{4,8},{8,4},{12,0},{1,13},{5,9},{9,5},{13,1},{2,14},{6,10},... | collective-permute-start | bytes 110600 | tf_op jit(solution)/shard_map/ppermute | solution.py:457
  8.6 0.0 collective-permute-start.1
  8.6 0.6 %collective-permute-start = (bf16[144,128]{1,0:T(8,128)(2,1)S(1)}, bf16[144,128]{1,0:T(8,128)(2,1)S(1)}, u32[]{:S(2)}, u32[]{:S(2)}) collective-permute-start(bf16[144,128]{1,0:T(8,128)(2,1)S(1)} %get-tuple-element.14.refs_0_), channel_id=1, source_target_pairs={{0,4},{4,0},{8,12},{12,8},{1,5},{5,1},{9,13},{13,9},{2,6},{6,2},{1... | collective-permute-start | bytes 110600 | tf_op jit(solution)/shard_map/ppermute | solution.py:457
  9.9 0.9 %collective-permute-done.2.refs_3_ = bf16[144,128]{1,0:T(8,128)(2,1)S(1)} collective-permute-done((bf16[144,128]{1,0:T(8,128)(2,1)S(1)}, bf16[144,128]{1,0:T(8,128)(2,1)S(1)}, u32[]{:S(2)}, u32[]{:S(2)}) %collective-permute-start.2) | collective-permute-done | bytes 36896 | tf_op jit(solution)/shard_map/ppermute | solution.py:457
  10.8 2.7 %collective-permute-done.1.refs_2_ = bf16[144,128]{1,0:T(8,128)(2,1)S(1)} collective-permute-done((bf16[144,128]{1,0:T(8,128)(2,1)S(1)}, bf16[144,128]{1,0:T(8,128)(2,1)S(1)}, u32[]{:S(2)}, u32[]{:S(2)}) %collective-permute-start.1) | collective-permute-done | bytes 36896 | tf_op jit(solution)/shard_map/ppermute | solution.py:457
  13.5 0.0 collective-permute-done.refs_1_
  13.5 0.0 collective-permute-done.3.refs_6_.refs_5_
  13.6 0.0 copy-start
  13.6 0.0 copy-start.9
  13.6 0.0 copy-start.10
  13.6 0.0 copy-start.12
  13.6 2.0 %shard_map.183 = bf16[16,16,128]{2,1,0:T(8,128)(2,1)S(1)} custom-call(s32[3,16]{1,0:T(4,128)S(4)} %get-tuple-element.13.table, f32[1]{0:T(128)S(6)} %copy.21.dose, bf16[144,128]{1,0:T(8,128)(2,1)S(1)} %get-tuple-element.14.refs_0_, bf16[144,128]{1,0:T(8,128)(2,1)S(1)} %collective-permute-done.refs_1_, bf16[144,128]{1,0:T(8,128)(2,1)S(1)} %collective-permute-done.1.refs_2_, ...), custom_call_target="tpu_custom_call" | custom-call | tf_op jit(solution)/shard_map/pallas_call | solution.py:427
  15.6 0.0 copy-start.4
  15.6 0.0 copy-start.6
  15.6 11.2 %all_to_all.10.grads = bf16[16,16,128]{2,1,0:T(8,128)(2,1)S(1)} all-to-all(bf16[16,16,128]{2,1,0:T(8,128)(2,1)S(1)} %shard_map.183), channel_id=1, replica_groups=mesh['groups'=2,'cells'=4,'corners'=2,'kern'=2] {'cells','corners','kern'}, dimensions={0} | all-to-all | bytes 131072 | tf_op jit(solution)/shard_map/all_to_all | solution.py:514
  26.8 1.6 %shard_map.184 = (f32[8,128,128]{2,1,0:T(8,128)S(1)}, f32[8,8,256]{2,1,0:T(8,128)S(1)}, bf16[16,128]{1,0:T(8,128)(2,1)S(1)}, bf16[16,128]{1,0:T(8,128)(2,1)S(1)}...) custom-call(f32[8,128,128]{2,1,0:T(8,128)S(1)} %copy-done, bf16[16,16,128]{2,1,0:T(8,128)(2,1)S(1)} %all_to_all.10.grads, ...), custom_call_target="tpu_custom_call" | custom-call | tf_op jit(solution)/shard_map/pallas_call | solution.py:427
  28.4 0.2 collective-permute-start.4
  28.6 1.0 %collective-permute-start.5 = (bf16[16,128]{1,0:T(8,128)(2,1)S(1)}, bf16[16,128]{1,0:T(8,128)(2,1)S(1)}, u32[]{:S(2)}, u32[]{:S(2)}) collective-permute-start(bf16[16,128]{1,0:T(8,128)(2,1)S(1)} %get-tuple-element.18), channel_id=1, source_target_pairs={{0,8},{4,12},{8,0},{12,4},{1,9},{5,13},{9,1},{13,5},{2,10},{6,14},... | collective-permute-start | bytes 12296 | tf_op jit(solution)/shard_map/ppermute | solution.py:457
  29.6 3.3 %collective-permute-start.6 = (bf16[16,128]{1,0:T(8,128)(2,1)S(1)}, bf16[16,128]{1,0:T(8,128)(2,1)S(1)}, u32[]{:S(2)}, u32[]{:S(2)}) collective-permute-start(bf16[16,128]{1,0:T(8,128)(2,1)S(1)} %get-tuple-element.19), channel_id=1, source_target_pairs={{0,12},{4,8},{8,4},{12,0},{1,13},{5,9},{9,5},{13,1},{2,14},{6,10},... | collective-permute-start | bytes 12296 | tf_op jit(solution)/shard_map/ppermute | solution.py:457
  32.8 0.2 collective-permute-done.5.refs_2_
  33.1 1.9 %collective-permute-done.6.refs_3_ = bf16[16,128]{1,0:T(8,128)(2,1)S(1)} collective-permute-done((bf16[16,128]{1,0:T(8,128)(2,1)S(1)}, bf16[16,128]{1,0:T(8,128)(2,1)S(1)}, u32[]{:S(2)}, u32[]{:S(2)}) %collective-permute-start.6) | collective-permute-done | bytes 4128 | tf_op jit(solution)/shard_map/ppermute | solution.py:457
  35.0 1.9 %shard_map.185 = bf16[16,16,128]{2,1,0:T(8,128)(2,1)S(1)} custom-call(f32[1]{0:T(128)S(6)} %copy.21.dose, bf16[16,128]{1,0:T(8,128)(2,1)S(1)} %get-tuple-element.16.refs_0_, bf16[16,128]{1,0:T(8,128)(2,1)S(1)} %collective-permute-done.4.refs_1_, bf16[16,128]{1,0:T(8,128)(2,1)S(1)} %collective-permute-done.5.refs_2_, ...), custom_call_target="tpu_custom_call" | custom-call | tf_op jit(solution)/shard_map/pallas_call | solution.py:427
  36.8 11.3 %all_to_all.11.grads = bf16[16,16,128]{2,1,0:T(8,128)(2,1)S(1)} all-to-all(bf16[16,16,128]{2,1,0:T(8,128)(2,1)S(1)} %shard_map.185), channel_id=1, replica_groups=mesh['groups'=2,'cells'=4,'corners'=2,'kern'=2] {'cells','corners','kern'}, dimensions={0} | all-to-all | bytes 131072 | tf_op jit(solution)/shard_map/all_to_all | solution.py:533
  48.2 1.3 %shard_map.186 = f32[8,32,128]{2,1,0:T(8,128)} custom-call(f32[8,128,128]{2,1,0:T(8,128)S(1)} %get-tuple-element.15.theta, bf16[16,16,128]{2,1,0:T(8,128)(2,1)S(1)} %all_to_all.11.grads, f32[8,8,256]{2,1,0:T(8,128)S(1)} %get-tuple-element.20.sums, bf16[128,256]{1,0:T(8,128)(2,1)S(1)} %copy-done.4, bf16[128,48]{1,0:T(8,128)(2,1)S(1)} %copy-done.9), custom_call_target="tpu_custom_call" | custom-call | tf_op jit(solution)/shard_map/pallas_call | solution.py:427
  (19 shorter events, 0.0 us)
Async XLA Ops:
  1.0 12.4 %copy-start.13 = (bf16[72,128]{1,0:T(8,128)(2,1)S(1)}, bf16[72,128]{1,0:T(8,128)(2,1)}, u32[]{:S(2)}) copy-start(bf16[72,128]{1,0:T(8,128)(2,1)} %constant.32.clone.refs_13_.refs_12_) | copy-start | bytes 55300
  1.4 12.0 %collective-permute-start.3 = (bf16[12,48,128]{2,1,0:T(8,128)(2,1)S(1)}, bf16[12,48,128]{2,1,0:T(8,128)(2,1)S(1)}, u32[]{:S(2)}, u32[]{:S(2)}) collective-permute-start(bf16[12,48,128]{2,1,0:T(8,128)(2,1)S(1)} %shard_map.182.refs_5_.refs_4_), channel_id=1, source_target_pairs={{0,1},{1,0},{2,3},{3,2},{4,5},{5,4},{6,7},{7,6},{8,9},{9,8},{10,11... | collective-permute-start | bytes 442376 | tf_op jit(solution)/shard_map/ppermute | solution.py:457
  2.0 11.5 %copy-start.1 = (bf16[256,256]{1,0:T(8,128)(2,1)S(1)}, bf16[256,256]{1,0:T(8,128)(2,1)}, u32[]{:S(2)}) copy-start(bf16[256,256]{1,0:T(8,128)(2,1)} %constant.28.clone.refs_9_.refs_8_) | copy-start | bytes 393220
  2.0 11.5 %copy-start.2 = (bf16[256,256]{1,0:T(8,128)(2,1)S(1)}, bf16[256,256]{1,0:T(8,128)(2,1)}, u32[]{:S(2)}) copy-start(bf16[256,256]{1,0:T(8,128)(2,1)} %constant.27.clone.refs_8_.refs_7_) | copy-start | bytes 393220
  2.0 11.5 %copy-start.3 = (bf16[2,128,128]{2,1,0:T(8,128)(2,1)S(1)}, bf16[2,128,128]{2,1,0:T(8,128)(2,1)}, u32[]{:S(2)}) copy-start(bf16[2,128,128]{2,1,0:T(8,128)(2,1)} %refs_6_.1) | copy-start | bytes 196612
  2.0 11.5 %copy-start.5 = (bf16[128,224]{1,0:T(8,128)(2,1)S(1)}, bf16[128,224]{1,0:T(8,128)(2,1)}, u32[]{:S(2)}) copy-start(bf16[128,224]{1,0:T(8,128)(2,1)} %constant.31.clone.refs_12_.refs_11_) | copy-start | bytes 172036
  2.0 11.5 %copy-start.7 = (bf16[96,144]{1,0:T(8,128)(2,1)S(1)}, bf16[96,144]{1,0:T(8,128)(2,1)}, u32[]{:S(2)}) copy-start(bf16[96,144]{1,0:T(8,128)(2,1)} %constant.30.clone.refs_11_.refs_10_) | copy-start | bytes 82948
  2.0 11.5 %copy-start.8 = (bf16[144,96]{1,0:T(8,128)(2,1)S(1)}, bf16[144,96]{1,0:T(8,128)(2,1)}, u32[]{:S(2)}) copy-start(bf16[144,96]{1,0:T(8,128)(2,1)} %constant.29.clone.refs_10_.refs_9_) | copy-start | bytes 82948
  2.0 11.5 %copy-start.11 = (f32[128,256]{1,0:T(8,128)S(1)}, f32[128,256]{1,0:T(8,128)}, u32[]{:S(2)}) copy-start(f32[128,256]{1,0:T(8,128)} %constant.26.clone.refs_4_) | copy-start | bytes 393220
  3.9 6.9 %collective-permute-start.2 = (bf16[144,128]{1,0:T(8,128)(2,1)S(1)}, bf16[144,128]{1,0:T(8,128)(2,1)S(1)}, u32[]{:S(2)}, u32[]{:S(2)}) collective-permute-start(bf16[144,128]{1,0:T(8,128)(2,1)S(1)} %get-tuple-element.14.refs_0_), channel_id=1, source_target_pairs={{0,12},{4,8},{8,4},{12,0},{1,13},{5,9},{9,5},{13,1},{2,14},{6,10},... | collective-permute-start | bytes 110600 | tf_op jit(solution)/shard_map/ppermute | solution.py:457
  8.6 4.9 %collective-permute-start.1 = (bf16[144,128]{1,0:T(8,128)(2,1)S(1)}, bf16[144,128]{1,0:T(8,128)(2,1)S(1)}, u32[]{:S(2)}, u32[]{:S(2)}) collective-permute-start(bf16[144,128]{1,0:T(8,128)(2,1)S(1)} %get-tuple-element.14.refs_0_), channel_id=1, source_target_pairs={{0,8},{4,12},{8,0},{12,4},{1,9},{5,13},{9,1},{13,5},{2,10},{6,14},... | collective-permute-start | bytes 110600 | tf_op jit(solution)/shard_map/ppermute | solution.py:457
  8.6 4.9 %collective-permute-start = (bf16[144,128]{1,0:T(8,128)(2,1)S(1)}, bf16[144,128]{1,0:T(8,128)(2,1)S(1)}, u32[]{:S(2)}, u32[]{:S(2)}) collective-permute-start(bf16[144,128]{1,0:T(8,128)(2,1)S(1)} %get-tuple-element.14.refs_0_), channel_id=1, source_target_pairs={{0,4},{4,0},{8,12},{12,8},{1,5},{5,1},{9,13},{13,9},{2,6},{6,2},{1... | collective-permute-start | bytes 110600 | tf_op jit(solution)/shard_map/ppermute | solution.py:457
  13.6 13.2 %copy-start = (f32[8,128,128]{2,1,0:T(8,128)S(1)}, f32[8,128,128]{2,1,0:T(8,128)}, u32[]{:S(2)}) copy-start(f32[8,128,128]{2,1,0:T(8,128)} %theta.3) | copy-start | bytes 1572868
  13.6 13.2 %copy-start.9 = (bf16[128,48]{1,0:T(8,128)(2,1)S(1)}, bf16[128,48]{1,0:T(8,128)(2,1)}, u32[]{:S(2)}) copy-start(bf16[128,48]{1,0:T(8,128)(2,1)} %constant.35.clone.ex) | copy-start | bytes 36868
  13.6 13.2 %copy-start.10 = (bf16[128,512]{1,0:T(8,128)(2,1)S(1)}, bf16[128,512]{1,0:T(8,128)(2,1)}, u32[]{:S(2)}) copy-start(bf16[128,512]{1,0:T(8,128)(2,1)} %constant.33.clone.ph) | copy-start | bytes 393220
  13.6 13.2 %copy-start.12 = (bf16[96,128]{1,0:T(8,128)(2,1)S(1)}, bf16[96,128]{1,0:T(8,128)(2,1)}, u32[]{:S(2)}) copy-start(bf16[96,128]{1,0:T(8,128)(2,1)} %constant.25.clone.fx) | copy-start | bytes 73732
  15.6 11.2 %copy-start.4 = (bf16[128,256]{1,0:T(8,128)(2,1)S(1)}, bf16[128,256]{1,0:T(8,128)(2,1)}, u32[]{:S(2)}) copy-start(bf16[128,256]{1,0:T(8,128)(2,1)} %constant.34.clone.gy) | copy-start | bytes 196612
  15.6 11.2 %copy-start.6 = (bf16[128,256]{1,0:T(8,128)(2,1)S(1)}, bf16[128,256]{1,0:T(8,128)(2,1)}, u32[]{:S(2)}) copy-start(bf16[128,256]{1,0:T(8,128)(2,1)} %constant.24.clone.fy) | copy-start | bytes 196612
  28.4 4.4 %collective-permute-start.4 = (bf16[16,128]{1,0:T(8,128)(2,1)S(1)}, bf16[16,128]{1,0:T(8,128)(2,1)S(1)}, u32[]{:S(2)}, u32[]{:S(2)}) collective-permute-start(bf16[16,128]{1,0:T(8,128)(2,1)S(1)} %get-tuple-element.17), channel_id=1, source_target_pairs={{0,4},{4,0},{8,12},{12,8},{1,5},{5,1},{9,13},{13,9},{2,6},{6,2},{1... | collective-permute-start | bytes 12296 | tf_op jit(solution)/shard_map/ppermute | solution.py:457
  28.6 4.5 %collective-permute-start.5 = (bf16[16,128]{1,0:T(8,128)(2,1)S(1)}, bf16[16,128]{1,0:T(8,128)(2,1)S(1)}, u32[]{:S(2)}, u32[]{:S(2)}) collective-permute-start(bf16[16,128]{1,0:T(8,128)(2,1)S(1)} %get-tuple-element.18), channel_id=1, source_target_pairs={{0,8},{4,12},{8,0},{12,4},{1,9},{5,13},{9,1},{13,5},{2,10},{6,14},... | collective-permute-start | bytes 12296 | tf_op jit(solution)/shard_map/ppermute | solution.py:457
  29.6 5.4 %collective-permute-start.6 = (bf16[16,128]{1,0:T(8,128)(2,1)S(1)}, bf16[16,128]{1,0:T(8,128)(2,1)S(1)}, u32[]{:S(2)}, u32[]{:S(2)}) collective-permute-start(bf16[16,128]{1,0:T(8,128)(2,1)S(1)} %get-tuple-element.19), channel_id=1, source_target_pairs={{0,12},{4,8},{8,4},{12,0},{1,13},{5,9},{9,5},{13,1},{2,14},{6,10},... | collective-permute-start | bytes 12296 | tf_op jit(solution)/shard_map/ppermute | solution.py:457
where the time goes:
time: 49.8 us; the launch traced here: 49.5 us
  blocking collectives  22.5 us (45%)
  starting transfers between devices  10.3 us (21%)
  Pallas kernels  9.01 us (18%)
  waiting for transfers between devices  5.71 us (11%)
  local copies, waits for them, and re-layouts  1.13 us (2%)
  between operations  0.84 us (2%)
    all_to_all x2, blocking collectives, per_device(): grads = lax.all_to_all(grads, everyone, 0, 0, tiled=True)  22.5 us
    ppermute x7, starting transfers between devices, shifted(): return lax.ppermute(array, axis, moves)  10.3 us
    pallas_call x6, Pallas kernels, call(): pl.pallas_call(body, out_shape=outs, in_specs=[SMEM] * len(scalars) + [VM...  9.01 us
    ppermute x7, waiting for transfers between devices, shifted(): return lax.ppermute(array, axis, moves)  5.71 us
    unnamed x29, local copies, waits for them, and re-layouts  1.13 us
  transfers between devices with their start and end apart: 7, of which 4 were waited for; matrix products, arithmetic and copies ran while one was open for 0% of the time, Pallas kernels for 4%

commit v1 on v0

--- a/solution.py
+++ b/solution.py
@@ -64,12 +64,13 @@
         both = np.concatenate([gy, np.roll(gy, HALF, axis=0)], axis=0)
         self.gyy = both.astype(np.float32).astype(BF)
         self.gyy_t = self.gyy.T.copy()
-        gx = np.zeros((2 * grid, 4 * rows))
+        self.span = up(2 * mid + 1, 8)
         phase = (f[None, :] * np.arange(grid)[:, None] % grid) * (2.0 * np.pi / grid)
-        cos, sin = np.zeros((grid, rows)), np.zeros((grid, rows))
-        cos[:, : mid + 1], sin[:, : mid + 1] = np.cos(phase), np.sin(phase)
-        gx[:grid] = np.concatenate([cos, cos, -sin, -sin], axis=1)
-        gx[grid:] = np.concatenate([sin, -sin, cos, -cos], axis=1)
+        blank = np.zeros((grid, self.span - 2 * mid - 1))
+        cos, sin = np.cos(phase), np.sin(phase)
+        upper = [cos, cos[:, 1:], blank, -sin, -sin[:, 1:], blank]
+        lower = [sin, -sin[:, 1:], blank, cos, -cos[:, 1:], blank]
+        gx = np.concatenate([np.concatenate(r, axis=1) for r in (upper, lower)], axis=0)
         self.gx = gx.astype(np.float32).astype(BF)
         self.gx_t = self.gx.T.copy()
         u = np.arange(-2 * mid, 2 * mid + 1)
@@ -155,7 +156,7 @@
 
 
 def arrange_body(tabs, kern, out):
-    freq, mid, rows = tabs.freq, tabs.mid, tabs.rows
+    freq, mid, span = tabs.freq, tabs.mid, tabs.span
     number, tall = out.shape[0], up(freq, 8)
     side = jnp.zeros((freq, HALF - freq), F32)
     below = jnp.zeros((tall - freq, LANES), F32)
@@ -170,10 +171,10 @@
     turned = jnp.where(same, jnp.where(row < HALF, 1.0, -1.0), 0.0).astype(BF)
     lefts = dot(rights, turned)
     rights = rights.astype(F32)
-    row = lax.broadcasted_iota(jnp.int32, (2 * rows, 2 * tall), 0)
-    col = lane_of((2 * rows, 2 * tall))
+    row = lax.broadcasted_iota(jnp.int32, (span, 2 * tall), 0)
+    col = lane_of((span, 2 * tall))
     upper = (row <= mid) & (col == mid + row)
-    lower = (row > rows) & (row <= rows + mid) & (col == tall + mid - (row - rows))
+    lower = (row > mid) & (row <= 2 * mid) & (col == tall + 2 * mid - row)
     pick = jnp.where(upper | lower, 1.0, 0.0).astype(BF)
     for k in range(0, number, 2):
         columns = [
@@ -182,9 +183,9 @@
             )
             for m in range(k, min(k + 2, number))
         ]
-        res = dot(pick, jnp.concatenate(columns, axis=1).astype(BF)).astype(BF)
+        res = dot(pick, jnp.concatenate(columns, axis=1).astype(BF))
         for p in range(len(columns)):
-            out[k + p] = res[:, p * LANES : (p + 1) * LANES]
+            out[k + p] = res[:, p * LANES : (p + 1) * LANES].astype(BF)
 
 
 def spectra(tabs, slots, theta, fy, fx):
@@ -283,16 +284,19 @@
     other = swap(spec)
     real = jnp.where(left, spec, other)
     imag = jnp.where(left, other, -spec)
-    real = jnp.concatenate([real, real], axis=0)
-    imag = jnp.concatenate([imag, imag], axis=0)
+    span, mid = tabs.span, tabs.mid
+    rest = jnp.zeros((span - rows, LANES), F32)
+    upper = lax.broadcasted_iota(jnp.int32, (span, LANES), 0) <= mid
+    real, imag = [jnp.concatenate([part, rest], axis=0) for part in (real, imag)]
+    real, imag = [jnp.where(upper, part, pltpu.roll(part, mid, 0)) for part in (real, imag)]
     wanted = target[lax.axis_index("kern")].astype(F32)
-    span = 2 * rows
     members = [(ref, k) for ref in arranged for k in range(ref.shape[0])]
     number = len(members)
-    for m, (ref, k) in enumerate(members):
-        kern = ref[k].astype(F32)
-        wide[m * span : (m + 1) * span, :LANES] = (kern * real).astype(BF)
-        wide[m * span : (m + 1) * span, LANES:] = (kern * imag).astype(BF)
+    for m in range(0, number, 2):
+        kerns = [ref[k].astype(F32) for ref, k in members[m : m + 2]]
+        lines = slice(m * span, (m + len(kerns)) * span)
+        wide[lines, :LANES] = jnp.concatenate([k * real for k in kerns], axis=0).astype(BF)
+        wide[lines, LANES:] = jnp.concatenate([k * imag for k in kerns], axis=0).astype(BF)
     for first in range(0, number, CHUNK):
         last = min(first + CHUNK, number)
         res = dot(wide[first * span : last * span], gyy[...])
@@ -320,11 +324,11 @@
         for p in range(min(2, number - m)):
             one = near[m + p]
             pair.append(jnp.concatenate([one[:grid] * push, one[grid:] * push], axis=0))
-        back = dot(gx_t[...], jnp.concatenate(pair, axis=1).astype(BF)).astype(BF)
-        for p in range(len(pair)):
-            at_row = (m + p) * span
-            wide[at_row : at_row + span, :LANES] = back[:span, p * cell : (p + 1) * cell]
-            wide[at_row : at_row + span, LANES:] = back[span:, p * cell : (p + 1) * cell]
+        back = dot(gx_t[...], jnp.concatenate(pair, axis=1).astype(BF))
+        lines = slice(m * span, (m + len(pair)) * span)
+        halves = [back[:, p * cell : (p + 1) * cell] for p in range(len(pair))]
+        wide[lines, :LANES] = jnp.concatenate([h[:span] for h in halves], axis=0).astype(BF)
+        wide[lines, LANES:] = jnp.concatenate([h[span:] for h in halves], axis=0).astype(BF)
     sum_real = jnp.zeros((span, LANES), F32)
     sum_imag = jnp.zeros((span, LANES), F32)
     for first in range(0, number, CHUNK):
@@ -336,8 +340,11 @@
             part = res[(m - first) * span : (m - first + 1) * span]
             sum_real = sum_real + kern * part[:, :LANES]
             sum_imag = sum_imag + kern * part[:, LANES:]
-    sum_real = sum_real[:rows] + sum_real[rows:]
-    sum_imag = sum_imag[:rows] + sum_imag[rows:]
+    sums = []
+    for part in (sum_real, sum_imag):
+        below = pltpu.roll(jnp.where(upper, 0.0, part), span - mid, 0)
+        sums.append((jnp.where(upper, part, 0.0) + below)[:rows])
+    sum_real, sum_imag = sums
     grad = jnp.where(left, sum_real + swap(sum_real), swap(sum_imag - swap(sum_imag)))
     grad = pack(tabs, grad)
     for copy in range(copies):
@@ -467,7 +474,7 @@
     assert tiles == n_kern
     tabs = Tables(cell, kernels.shape[3])
     inst_owner = inst_owner[:, 0]
-    rows, sent = tabs.rows, packing(tabs)[0]
+    sent = packing(tabs)[0]
     band = cell // (n_kern * n_corners)
     payload, table = call(
         functools.partial(first_body, tabs, slots),
@@ -487,7 +494,7 @@
         functools.partial(arrange_body, tabs),
         [],
         [kernels],
-        shape((kernels.shape[2], 2 * rows, LANES), BF),
+        shape((kernels.shape[2], tabs.span, LANES), BF),
         name="arrange",
     )
     arranged = [own]
@@ -496,8 +503,8 @@
     copies = n * n_corners * n_kern
     count = n_kern * kernels.shape[2]
     scratch = [
-        pltpu.VMEM((count * 2 * rows, 2 * LANES), BF),
-        pltpu.VMEM((count, 4 * rows, cell), BF),
+        pltpu.VMEM((up(count, 2) * tabs.span, 2 * LANES), BF),
+        pltpu.VMEM((count, 2 * tabs.span, cell), BF),
         pltpu.VMEM((count, 2 * tabs.grid, cell), F32),
     ]
     common = arranged + [target, tabs.gyy, tabs.gyy_t, tabs.gx, tabs.gx_t, tabs.w, tabs.w_t]

time: 49.8 us -> 49.6 us (level)
  no operation moved by 1% of the time
where the time goes in v1:
time: 49.6 us; the launch traced here: 49.4 us
  blocking collectives  22.5 us (45%)
  starting transfers between devices  10.3 us (21%)
  Pallas kernels  8.87 us (18%)
  waiting for transfers between devices  5.71 us (12%)
  local copies, waits for them, and re-layouts  1.13 us (2%)
  between operations  0.84 us (2%)
    all_to_all x2, blocking collectives, per_device(): grads = lax.all_to_all(grads, everyone, 0, 0, tiled=True)  22.5 us
    ppermute x7, starting transfers between devices, shifted(): return lax.ppermute(array, axis, moves)  10.3 us
    pallas_call x6, Pallas kernels, call(): pl.pallas_call(body, out_shape=outs, in_specs=[SMEM] * len(scalars) + [VM...  8.87 us
    ppermute x7, waiting for transfers between devices, shifted(): return lax.ppermute(array, axis, moves)  5.71 us
    unnamed x29, local copies, waits for them, and re-layouts  1.13 us
  transfers between devices with their start and end apart: 7, of which 4 were waited for; matrix products, arithmetic and copies ran while one was open for 0% of the time, Pallas kernels for 4%

profile of v1, /device:TPU:0, one launch (start us, length us, event | category | flops | bytes accessed | tf_op | source)
XLA Modules:
  0.0 49.4 jit_solution(12918470028749521672)
XLA Ops:
  0.0 1.0 %copy.20.kern = f32[2,1,12,35,35]{4,3,2,1,0:T(8,128)S(1)} copy(f32[2,1,12,35,35]{4,1,3,2,0:T(1,128)} %param.21) | data formatting | bytes 235200 | tf_op args[2]
  1.0 0.4 shard_map.182.refs_5_.refs_4_
  1.4 0.6 %collective-permute-start.3 = (bf16[12,40,128]{2,1,0:T(8,128)(2,1)S(1)}, bf16[12,40,128]{2,1,0:T(8,128)(2,1)S(1)}, u32[]{:S(2)}, u32[]{:S(2)}) collective-permute-start(bf16[12,40,128]{2,1,0:T(8,128)(2,1)S(1)} %shard_map.182.refs_5_.refs_4_), channel_id=1, source_target_pairs={{0,1},{1,0},{2,3},{3,2},{4,5},{5,4},{6,7},{7,6},{8,9},{9,8},{10,11... | collective-permute-start | bytes 368648 | tf_op jit(solution)/shard_map/ppermute | solution.py:464
  2.0 0.0 copy-start.7
  2.0 0.0 copy-start.8
  2.0 0.0 copy-start.11
  2.0 0.0 copy-start.13
  2.1 1.9 %shard_map.181 = (bf16[144,128]{1,0:T(8,128)(2,1)S(1)}, s32[3,16]{1,0:T(4,128)S(4)}) custom-call(s32[16]{0:T(128)} %bitcast.1, s32[16]{0:T(128)} %local.1, s32[16]{0:T(128)} %shift.1, f32[8,128,128]{2,1,0:T(8,128)} %theta.3, bf16[128,256]{1,0:T(8,128)(2,1)} %constant.24.clone.fy, bf16[96,128]{1,0:T(8,128)(2,1)} %constant.25.clone.fx), custom_call_target="tpu_custom_call" | custom-call | tf_op jit(solution)/shard_map/pallas_call | solution.py:434
  3.9 4.7 %collective-permute-start.2 = (bf16[144,128]{1,0:T(8,128)(2,1)S(1)}, bf16[144,128]{1,0:T(8,128)(2,1)S(1)}, u32[]{:S(2)}, u32[]{:S(2)}) collective-permute-start(bf16[144,128]{1,0:T(8,128)(2,1)S(1)} %get-tuple-element.14.refs_0_), channel_id=1, source_target_pairs={{0,12},{4,8},{8,4},{12,0},{1,13},{5,9},{9,5},{13,1},{2,14},{6,10},... | collective-permute-start | bytes 110600 | tf_op jit(solution)/shard_map/ppermute | solution.py:464
  8.6 0.0 collective-permute-start.1
  8.6 0.6 %collective-permute-start = (bf16[144,128]{1,0:T(8,128)(2,1)S(1)}, bf16[144,128]{1,0:T(8,128)(2,1)S(1)}, u32[]{:S(2)}, u32[]{:S(2)}) collective-permute-start(bf16[144,128]{1,0:T(8,128)(2,1)S(1)} %get-tuple-element.14.refs_0_), channel_id=1, source_target_pairs={{0,4},{4,0},{8,12},{12,8},{1,5},{5,1},{9,13},{13,9},{2,6},{6,2},{1... | collective-permute-start | bytes 110600 | tf_op jit(solution)/shard_map/ppermute | solution.py:464
  9.9 0.9 %collective-permute-done.2.refs_3_ = bf16[144,128]{1,0:T(8,128)(2,1)S(1)} collective-permute-done((bf16[144,128]{1,0:T(8,128)(2,1)S(1)}, bf16[144,128]{1,0:T(8,128)(2,1)S(1)}, u32[]{:S(2)}, u32[]{:S(2)}) %collective-permute-start.2) | collective-permute-done | bytes 36896 | tf_op jit(solution)/shard_map/ppermute | solution.py:464
  10.8 2.7 %collective-permute-done.1.refs_2_ = bf16[144,128]{1,0:T(8,128)(2,1)S(1)} collective-permute-done((bf16[144,128]{1,0:T(8,128)(2,1)S(1)}, bf16[144,128]{1,0:T(8,128)(2,1)S(1)}, u32[]{:S(2)}, u32[]{:S(2)}) %collective-permute-start.1) | collective-permute-done | bytes 36896 | tf_op jit(solution)/shard_map/ppermute | solution.py:464
  13.5 0.0 collective-permute-done.refs_1_
  13.6 0.0 copy-start
  13.6 0.0 copy-start.9
  13.6 0.0 copy-start.10
  13.6 0.0 copy-start.12
  13.6 1.9 %shard_map.183 = bf16[16,16,128]{2,1,0:T(8,128)(2,1)S(1)} custom-call(s32[3,16]{1,0:T(4,128)S(4)} %get-tuple-element.13.table, f32[1]{0:T(128)S(6)} %copy.21.dose, bf16[144,128]{1,0:T(8,128)(2,1)S(1)} %get-tuple-element.14.refs_0_, bf16[144,128]{1,0:T(8,128)(2,1)S(1)} %collective-permute-done.refs_1_, bf16[144,128]{1,0:T(8,128)(2,1)S(1)} %collective-permute-done.1.refs_2_, ...), custom_call_target="tpu_custom_call" | custom-call | tf_op jit(solution)/shard_map/pallas_call | solution.py:434
  15.5 0.0 copy-start.3
  15.5 0.0 copy-start.4
  15.6 11.1 %all_to_all.10.grads = bf16[16,16,128]{2,1,0:T(8,128)(2,1)S(1)} all-to-all(bf16[16,16,128]{2,1,0:T(8,128)(2,1)S(1)} %shard_map.183), channel_id=1, replica_groups=mesh['groups'=2,'cells'=4,'corners'=2,'kern'=2] {'cells','corners','kern'}, dimensions={0} | all-to-all | bytes 131072 | tf_op jit(solution)/shard_map/all_to_all | solution.py:521
  26.7 1.6 %shard_map.184 = (f32[8,128,128]{2,1,0:T(8,128)S(1)}, f32[8,8,256]{2,1,0:T(8,128)S(1)}, bf16[16,128]{1,0:T(8,128)(2,1)S(1)}, bf16[16,128]{1,0:T(8,128)(2,1)S(1)}...) custom-call(f32[8,128,128]{2,1,0:T(8,128)S(1)} %copy-done, bf16[16,16,128]{2,1,0:T(8,128)(2,1)S(1)} %all_to_all.10.grads, ...), custom_call_target="tpu_custom_call" | custom-call | tf_op jit(solution)/shard_map/pallas_call | solution.py:434
  28.3 0.2 collective-permute-start.4
  28.5 1.0 %collective-permute-start.5 = (bf16[16,128]{1,0:T(8,128)(2,1)S(1)}, bf16[16,128]{1,0:T(8,128)(2,1)S(1)}, u32[]{:S(2)}, u32[]{:S(2)}) collective-permute-start(bf16[16,128]{1,0:T(8,128)(2,1)S(1)} %get-tuple-element.18), channel_id=1, source_target_pairs={{0,8},{4,12},{8,0},{12,4},{1,9},{5,13},{9,1},{13,5},{2,10},{6,14},... | collective-permute-start | bytes 12296 | tf_op jit(solution)/shard_map/ppermute | solution.py:464
  29.5 3.3 %collective-permute-start.6 = (bf16[16,128]{1,0:T(8,128)(2,1)S(1)}, bf16[16,128]{1,0:T(8,128)(2,1)S(1)}, u32[]{:S(2)}, u32[]{:S(2)}) collective-permute-start(bf16[16,128]{1,0:T(8,128)(2,1)S(1)} %get-tuple-element.19), channel_id=1, source_target_pairs={{0,12},{4,8},{8,4},{12,0},{1,13},{5,9},{9,5},{13,1},{2,14},{6,10},... | collective-permute-start | bytes 12296 | tf_op jit(solution)/shard_map/ppermute | solution.py:464
  32.8 0.0 collective-permute-done.4.refs_1_
  32.8 0.2 collective-permute-done.5.refs_2_
  33.0 1.9 %collective-permute-done.6.refs_3_ = bf16[16,128]{1,0:T(8,128)(2,1)S(1)} collective-permute-done((bf16[16,128]{1,0:T(8,128)(2,1)S(1)}, bf16[16,128]{1,0:T(8,128)(2,1)S(1)}, u32[]{:S(2)}, u32[]{:S(2)}) %collective-permute-start.6) | collective-permute-done | bytes 4128 | tf_op jit(solution)/shard_map/ppermute | solution.py:464
  34.9 1.8 %shard_map.185 = bf16[16,16,128]{2,1,0:T(8,128)(2,1)S(1)} custom-call(f32[1]{0:T(128)S(6)} %copy.21.dose, bf16[16,128]{1,0:T(8,128)(2,1)S(1)} %get-tuple-element.16.refs_0_, bf16[16,128]{1,0:T(8,128)(2,1)S(1)} %collective-permute-done.4.refs_1_, bf16[16,128]{1,0:T(8,128)(2,1)S(1)} %collective-permute-done.5.refs_2_, ...), custom_call_target="tpu_custom_call" | custom-call | tf_op jit(solution)/shard_map/pallas_call | solution.py:434
  36.7 11.3 %all_to_all.11.grads = bf16[16,16,128]{2,1,0:T(8,128)(2,1)S(1)} all-to-all(bf16[16,16,128]{2,1,0:T(8,128)(2,1)S(1)} %shard_map.185), channel_id=1, replica_groups=mesh['groups'=2,'cells'=4,'corners'=2,'kern'=2] {'cells','corners','kern'}, dimensions={0} | all-to-all | bytes 131072 | tf_op jit(solution)/shard_map/all_to_all | solution.py:540
  48.0 1.3 %shard_map.186 = f32[8,32,128]{2,1,0:T(8,128)} custom-call(f32[8,128,128]{2,1,0:T(8,128)S(1)} %get-tuple-element.15.theta, bf16[16,16,128]{2,1,0:T(8,128)(2,1)S(1)} %all_to_all.11.grads, f32[8,8,256]{2,1,0:T(8,128)S(1)} %get-tuple-element.20.sums, bf16[128,256]{1,0:T(8,128)(2,1)S(1)} %copy-done.3, bf16[128,48]{1,0:T(8,128)(2,1)S(1)} %copy-done.9), custom_call_target="tpu_custom_call" | custom-call | tf_op jit(solution)/shard_map/pallas_call | solution.py:434
  (19 shorter events, 0.0 us)
Async XLA Ops:
  1.4 12.1 %collective-permute-start.3 = (bf16[12,40,128]{2,1,0:T(8,128)(2,1)S(1)}, bf16[12,40,128]{2,1,0:T(8,128)(2,1)S(1)}, u32[]{:S(2)}, u32[]{:S(2)}) collective-permute-start(bf16[12,40,128]{2,1,0:T(8,128)(2,1)S(1)} %shard_map.182.refs_5_.refs_4_), channel_id=1, source_target_pairs={{0,1},{1,0},{2,3},{3,2},{4,5},{5,4},{6,7},{7,6},{8,9},{9,8},{10,11... | collective-permute-start | bytes 368648 | tf_op jit(solution)/shard_map/ppermute | solution.py:464
  2.0 11.5 %copy-start.1 = (bf16[256,256]{1,0:T(8,128)(2,1)S(1)}, bf16[256,256]{1,0:T(8,128)(2,1)}, u32[]{:S(2)}) copy-start(bf16[256,256]{1,0:T(8,128)(2,1)} %constant.28.clone.refs_9_.refs_8_) | copy-start | bytes 393220
  2.0 11.5 %copy-start.2 = (bf16[256,256]{1,0:T(8,128)(2,1)S(1)}, bf16[256,256]{1,0:T(8,128)(2,1)}, u32[]{:S(2)}) copy-start(bf16[256,256]{1,0:T(8,128)(2,1)} %constant.27.clone.refs_8_.refs_7_) | copy-start | bytes 393220
  2.0 11.5 %copy-start.5 = (bf16[2,128,128]{2,1,0:T(8,128)(2,1)S(1)}, bf16[2,128,128]{2,1,0:T(8,128)(2,1)}, u32[]{:S(2)}) copy-start(bf16[2,128,128]{2,1,0:T(8,128)(2,1)} %refs_6_.1) | copy-start | bytes 196612
  2.0 11.5 %copy-start.6 = (bf16[128,224]{1,0:T(8,128)(2,1)S(1)}, bf16[128,224]{1,0:T(8,128)(2,1)}, u32[]{:S(2)}) copy-start(bf16[128,224]{1,0:T(8,128)(2,1)} %constant.31.clone.refs_12_.refs_11_) | copy-start | bytes 172036
  2.0 11.5 %copy-start.7 = (bf16[80,144]{1,0:T(8,128)(2,1)S(1)}, bf16[80,144]{1,0:T(8,128)(2,1)}, u32[]{:S(2)}) copy-start(bf16[80,144]{1,0:T(8,128)(2,1)} %constant.30.clone.refs_11_.refs_10_) | copy-start | bytes 69124
  2.0 11.5 %copy-start.8 = (bf16[144,80]{1,0:T(8,128)(2,1)S(1)}, bf16[144,80]{1,0:T(8,128)(2,1)}, u32[]{:S(2)}) copy-start(bf16[144,80]{1,0:T(8,128)(2,1)} %constant.29.clone.refs_10_.refs_9_) | copy-start | bytes 69124
  2.0 11.5 %copy-start.11 = (f32[128,256]{1,0:T(8,128)S(1)}, f32[128,256]{1,0:T(8,128)}, u32[]{:S(2)}) copy-start(f32[128,256]{1,0:T(8,128)} %constant.26.clone.refs_4_) | copy-start | bytes 393220
  2.0 11.5 %copy-start.13 = (bf16[72,128]{1,0:T(8,128)(2,1)S(1)}, bf16[72,128]{1,0:T(8,128)(2,1)}, u32[]{:S(2)}) copy-start(bf16[72,128]{1,0:T(8,128)(2,1)} %constant.32.clone.refs_13_.refs_12_) | copy-start | bytes 55300
  3.9 6.9 %collective-permute-start.2 = (bf16[144,128]{1,0:T(8,128)(2,1)S(1)}, bf16[144,128]{1,0:T(8,128)(2,1)S(1)}, u32[]{:S(2)}, u32[]{:S(2)}) collective-permute-start(bf16[144,128]{1,0:T(8,128)(2,1)S(1)} %get-tuple-element.14.refs_0_), channel_id=1, source_target_pairs={{0,12},{4,8},{8,4},{12,0},{1,13},{5,9},{9,5},{13,1},{2,14},{6,10},... | collective-permute-start | bytes 110600 | tf_op jit(solution)/shard_map/ppermute | solution.py:464
  8.6 4.9 %collective-permute-start.1 = (bf16[144,128]{1,0:T(8,128)(2,1)S(1)}, bf16[144,128]{1,0:T(8,128)(2,1)S(1)}, u32[]{:S(2)}, u32[]{:S(2)}) collective-permute-start(bf16[144,128]{1,0:T(8,128)(2,1)S(1)} %get-tuple-element.14.refs_0_), channel_id=1, source_target_pairs={{0,8},{4,12},{8,0},{12,4},{1,9},{5,13},{9,1},{13,5},{2,10},{6,14},... | collective-permute-start | bytes 110600 | tf_op jit(solution)/shard_map/ppermute | solution.py:464
  8.6 4.9 %collective-permute-start = (bf16[144,128]{1,0:T(8,128)(2,1)S(1)}, bf16[144,128]{1,0:T(8,128)(2,1)S(1)}, u32[]{:S(2)}, u32[]{:S(2)}) collective-permute-start(bf16[144,128]{1,0:T(8,128)(2,1)S(1)} %get-tuple-element.14.refs_0_), channel_id=1, source_target_pairs={{0,4},{4,0},{8,12},{12,8},{1,5},{5,1},{9,13},{13,9},{2,6},{6,2},{1... | collective-permute-start | bytes 110600 | tf_op jit(solution)/shard_map/ppermute | solution.py:464
  13.6 13.1 %copy-start = (f32[8,128,128]{2,1,0:T(8,128)S(1)}, f32[8,128,128]{2,1,0:T(8,128)}, u32[]{:S(2)}) copy-start(f32[8,128,128]{2,1,0:T(8,128)} %theta.3) | copy-start | bytes 1572868
  13.6 13.1 %copy-start.9 = (bf16[128,48]{1,0:T(8,128)(2,1)S(1)}, bf16[128,48]{1,0:T(8,128)(2,1)}, u32[]{:S(2)}) copy-start(bf16[128,48]{1,0:T(8,128)(2,1)} %constant.35.clone.ex) | copy-start | bytes 36868
  13.6 13.1 %copy-start.10 = (bf16[128,512]{1,0:T(8,128)(2,1)S(1)}, bf16[128,512]{1,0:T(8,128)(2,1)}, u32[]{:S(2)}) copy-start(bf16[128,512]{1,0:T(8,128)(2,1)} %constant.33.clone.ph) | copy-start | bytes 393220
  13.6 13.1 %copy-start.12 = (bf16[96,128]{1,0:T(8,128)(2,1)S(1)}, bf16[96,128]{1,0:T(8,128)(2,1)}, u32[]{:S(2)}) copy-start(bf16[96,128]{1,0:T(8,128)(2,1)} %constant.25.clone.fx) | copy-start | bytes 73732
  15.5 11.2 %copy-start.3 = (bf16[128,256]{1,0:T(8,128)(2,1)S(1)}, bf16[128,256]{1,0:T(8,128)(2,1)}, u32[]{:S(2)}) copy-start(bf16[128,256]{1,0:T(8,128)(2,1)} %constant.34.clone.gy) | copy-start | bytes 196612
  15.5 11.2 %copy-start.4 = (bf16[128,256]{1,0:T(8,128)(2,1)S(1)}, bf16[128,256]{1,0:T(8,128)(2,1)}, u32[]{:S(2)}) copy-start(bf16[128,256]{1,0:T(8,128)(2,1)} %constant.24.clone.fy) | copy-start | bytes 196612
  28.3 4.4 %collective-permute-start.4 = (bf16[16,128]{1,0:T(8,128)(2,1)S(1)}, bf16[16,128]{1,0:T(8,128)(2,1)S(1)}, u32[]{:S(2)}, u32[]{:S(2)}) collective-permute-start(bf16[16,128]{1,0:T(8,128)(2,1)S(1)} %get-tuple-element.17), channel_id=1, source_target_pairs={{0,4},{4,0},{8,12},{12,8},{1,5},{5,1},{9,13},{13,9},{2,6},{6,2},{1... | collective-permute-start | bytes 12296 | tf_op jit(solution)/shard_map/ppermute | solution.py:464
  28.5 4.5 %collective-permute-start.5 = (bf16[16,128]{1,0:T(8,128)(2,1)S(1)}, bf16[16,128]{1,0:T(8,128)(2,1)S(1)}, u32[]{:S(2)}, u32[]{:S(2)}) collective-permute-start(bf16[16,128]{1,0:T(8,128)(2,1)S(1)} %get-tuple-element.18), channel_id=1, source_target_pairs={{0,8},{4,12},{8,0},{12,4},{1,9},{5,13},{9,1},{13,5},{2,10},{6,14},... | collective-permute-start | bytes 12296 | tf_op jit(solution)/shard_map/ppermute | solution.py:464
  29.5 5.4 %collective-permute-start.6 = (bf16[16,128]{1,0:T(8,128)(2,1)S(1)}, bf16[16,128]{1,0:T(8,128)(2,1)S(1)}, u32[]{:S(2)}, u32[]{:S(2)}) collective-permute-start(bf16[16,128]{1,0:T(8,128)(2,1)S(1)} %get-tuple-element.19), channel_id=1, source_target_pairs={{0,12},{4,8},{8,4},{12,0},{1,13},{5,9},{9,5},{13,1},{2,14},{6,10},... | collective-permute-start | bytes 12296 | tf_op jit(solution)/shard_map/ppermute | solution.py:464

commit v2 on v1

--- a/solution.py
+++ b/solution.py
@@ -16,7 +16,7 @@
 LANES = 128
 HALF = LANES // 2
 INFO = 16
-CHUNK = 8
+CHUNK = 6
 BF = jnp.bfloat16
 F32 = jnp.float32
 
@@ -259,12 +259,15 @@
     for k in range(n):
         held[pl.ds(k * cells, cells)] = payload[k][0 : cells * sent].reshape(cells, sent, LANES)
     spec = jnp.zeros((tabs.rows, LANES), F32)
+    cross = spec
     for s in range(slots):
         i = j * slots + s
         which = source(n, z, table[0, i]) * cells + table[1, i]
         one = unpack(tabs, held[which])
         turn = ph[pl.ds(table[2, i], 1)]
-        spec = spec + one * turn[:, :LANES] + swap(one) * turn[:, LANES:]
+        spec = spec + one * turn[:, :LANES]
+        cross = cross + one * turn[:, LANES:]
+    spec = spec - swap(cross)
     tile_gradient(tabs, tiles, copies, spec, dose, rest, out, wide, tall, near)
 
 
@@ -360,13 +363,13 @@
         z, j = t // kern, t % kern
         parts = [grads[(z * corners + x) * kern + j].astype(F32) for x in range(corners)]
         own.append(unpack(tabs, sum(parts[1:], parts[0])))
-    swapped = [swap(grad) for grad in own]
     for c in range(cells):
-        total = jnp.zeros((rows, LANES), F32)
+        total, cross = jnp.zeros((rows, LANES), F32), jnp.zeros((rows, LANES), F32)
         for t in range(tiles):
             turn = sums[t, c : c + 1]
-            total = total + own[t] * turn[:, :LANES] - swapped[t] * turn[:, LANES:]
-        pieces.append(total * (2.0 / (slots * cell * cell)))
+            total = total + own[t] * turn[:, :LANES]
+            cross = cross + own[t] * turn[:, LANES:]
+        pieces.append((total + swap(cross)) * (2.0 / (slots * cell * cell)))
     rowed = dot(jnp.concatenate(pieces, axis=0).astype(BF), gy[...])
     result = []
     for first in range(0, cells, 2):
@@ -392,14 +395,16 @@
     ):
         out[c] = theta[c] - rate * gradient
     specs = spectra(tabs, slots, out[...], fy, fx)
-    swapped = [swap(spec) for spec in specs]
     z, j = lax.axis_index("cells"), lax.axis_index("kern")
     for k in range(n):
         turns = sums[target_of(n, z, k) * kern + j]
         total = jnp.zeros((tabs.rows, LANES), F32)
+        cross = total
         for c, spec in enumerate(specs):
             turn = turns[c : c + 1]
-            total = total + spec * turn[:, :LANES] + swapped[c] * turn[:, LANES:]
+            total = total + spec * turn[:, :LANES]
+            cross = cross + spec * turn[:, LANES:]
+        total = total - swap(cross)
         parts[k][...] = pack(tabs, total)
 
 

time: 49.6 us -> 49.5 us (level)
  no operation moved by 1% of the time
where the time goes in v2:
time: 49.5 us; the launch traced here: 49.2 us
  blocking collectives  22.5 us (45%)
  starting transfers between devices  10.3 us (21%)
  Pallas kernels  8.75 us (18%)
  waiting for transfers between devices  5.7 us (12%)
  local copies, waits for them, and re-layouts  1.12 us (2%)
  between operations  0.84 us (2%)
    all_to_all x2, blocking collectives, per_device(): grads = lax.all_to_all(grads, everyone, 0, 0, tiled=True)  22.5 us
    ppermute x7, starting transfers between devices, shifted(): return lax.ppermute(array, axis, moves)  10.3 us
    pallas_call x6, Pallas kernels, call(): pl.pallas_call(body, out_shape=outs, in_specs=[SMEM] * len(scalars) + [VM...  8.75 us
    ppermute x7, waiting for transfers between devices, shifted(): return lax.ppermute(array, axis, moves)  5.7 us
    unnamed x29, local copies, waits for them, and re-layouts  1.12 us
  transfers between devices with their start and end apart: 7, of which 4 were waited for; matrix products, arithmetic and copies ran while one was open for 0% of the time, Pallas kernels for 4%

profile of v2, /device:TPU:0, one launch (start us, length us, event | category | flops | bytes accessed | tf_op | source)
XLA Modules:
  0.0 49.2 jit_solution(11078870143587076598)
XLA Ops:
  0.0 1.0 %copy.20.kern = f32[2,1,12,35,35]{4,3,2,1,0:T(8,128)S(1)} copy(f32[2,1,12,35,35]{4,1,3,2,0:T(1,128)} %param.21) | data formatting | bytes 235200 | tf_op args[2]
  1.0 0.4 shard_map.182.refs_5_.refs_4_
  1.4 0.6 %collective-permute-start.3 = (bf16[12,40,128]{2,1,0:T(8,128)(2,1)S(1)}, bf16[12,40,128]{2,1,0:T(8,128)(2,1)S(1)}, u32[]{:S(2)}, u32[]{:S(2)}) collective-permute-start(bf16[12,40,128]{2,1,0:T(8,128)(2,1)S(1)} %shard_map.182.refs_5_.refs_4_), channel_id=1, source_target_pairs={{0,1},{1,0},{2,3},{3,2},{4,5},{5,4},{6,7},{7,6},{8,9},{9,8},{10,11... | collective-permute-start | bytes 368648 | tf_op jit(solution)/shard_map/ppermute | solution.py:469
  2.0 0.0 copy-start.7
  2.0 0.0 copy-start.8
  2.0 0.0 copy-start.11
  2.0 0.0 copy-start.13
  2.1 1.9 %shard_map.181 = (bf16[144,128]{1,0:T(8,128)(2,1)S(1)}, s32[3,16]{1,0:T(4,128)S(4)}) custom-call(s32[16]{0:T(128)} %bitcast.1, s32[16]{0:T(128)} %local.1, s32[16]{0:T(128)} %shift.1, f32[8,128,128]{2,1,0:T(8,128)} %theta.3, bf16[128,256]{1,0:T(8,128)(2,1)} %constant.24.clone.fy, bf16[96,128]{1,0:T(8,128)(2,1)} %constant.25.clone.fx), custom_call_target="tpu_custom_call" | custom-call | tf_op jit(solution)/shard_map/pallas_call | solution.py:439
  3.9 4.7 %collective-permute-start.2 = (bf16[144,128]{1,0:T(8,128)(2,1)S(1)}, bf16[144,128]{1,0:T(8,128)(2,1)S(1)}, u32[]{:S(2)}, u32[]{:S(2)}) collective-permute-start(bf16[144,128]{1,0:T(8,128)(2,1)S(1)} %get-tuple-element.14.refs_0_), channel_id=1, source_target_pairs={{0,12},{4,8},{8,4},{12,0},{1,13},{5,9},{9,5},{13,1},{2,14},{6,10},... | collective-permute-start | bytes 110600 | tf_op jit(solution)/shard_map/ppermute | solution.py:469
  8.6 0.0 collective-permute-start.1
  8.6 0.6 %collective-permute-start = (bf16[144,128]{1,0:T(8,128)(2,1)S(1)}, bf16[144,128]{1,0:T(8,128)(2,1)S(1)}, u32[]{:S(2)}, u32[]{:S(2)}) collective-permute-start(bf16[144,128]{1,0:T(8,128)(2,1)S(1)} %get-tuple-element.14.refs_0_), channel_id=1, source_target_pairs={{0,4},{4,0},{8,12},{12,8},{1,5},{5,1},{9,13},{13,9},{2,6},{6,2},{1... | collective-permute-start | bytes 110600 | tf_op jit(solution)/shard_map/ppermute | solution.py:469
  9.9 0.9 %collective-permute-done.2.refs_3_ = bf16[144,128]{1,0:T(8,128)(2,1)S(1)} collective-permute-done((bf16[144,128]{1,0:T(8,128)(2,1)S(1)}, bf16[144,128]{1,0:T(8,128)(2,1)S(1)}, u32[]{:S(2)}, u32[]{:S(2)}) %collective-permute-start.2) | collective-permute-done | bytes 36896 | tf_op jit(solution)/shard_map/ppermute | solution.py:469
  10.8 2.7 %collective-permute-done.1.refs_2_ = bf16[144,128]{1,0:T(8,128)(2,1)S(1)} collective-permute-done((bf16[144,128]{1,0:T(8,128)(2,1)S(1)}, bf16[144,128]{1,0:T(8,128)(2,1)S(1)}, u32[]{:S(2)}, u32[]{:S(2)}) %collective-permute-start.1) | collective-permute-done | bytes 36896 | tf_op jit(solution)/shard_map/ppermute | solution.py:469
  13.5 0.0 collective-permute-done.refs_1_
  13.5 0.0 collective-permute-done.3.refs_6_.refs_5_
  13.6 0.0 copy-start
  13.6 0.0 copy-start.9
  13.6 0.0 copy-start.10
  13.6 0.0 copy-start.12
  13.6 1.9 %shard_map.183 = bf16[16,16,128]{2,1,0:T(8,128)(2,1)S(1)} custom-call(s32[3,16]{1,0:T(4,128)S(4)} %get-tuple-element.13.table, f32[1]{0:T(128)S(6)} %copy.21.dose, bf16[144,128]{1,0:T(8,128)(2,1)S(1)} %get-tuple-element.14.refs_0_, bf16[144,128]{1,0:T(8,128)(2,1)S(1)} %collective-permute-done.refs_1_, bf16[144,128]{1,0:T(8,128)(2,1)S(1)} %collective-permute-done.1.refs_2_, ...), custom_call_target="tpu_custom_call" | custom-call | tf_op jit(solution)/shard_map/pallas_call | solution.py:439
  15.5 0.0 copy-start.3
  15.5 0.0 copy-start.4
  15.5 11.2 %all_to_all.10.grads = bf16[16,16,128]{2,1,0:T(8,128)(2,1)S(1)} all-to-all(bf16[16,16,128]{2,1,0:T(8,128)(2,1)S(1)} %shard_map.183), channel_id=1, replica_groups=mesh['groups'=2,'cells'=4,'corners'=2,'kern'=2] {'cells','corners','kern'}, dimensions={0} | all-to-all | bytes 131072 | tf_op jit(solution)/shard_map/all_to_all | solution.py:526
  26.7 1.6 %shard_map.184 = (f32[8,128,128]{2,1,0:T(8,128)S(1)}, f32[8,8,256]{2,1,0:T(8,128)S(1)}, bf16[16,128]{1,0:T(8,128)(2,1)S(1)}, bf16[16,128]{1,0:T(8,128)(2,1)S(1)}...) custom-call(f32[8,128,128]{2,1,0:T(8,128)S(1)} %copy-done, bf16[16,16,128]{2,1,0:T(8,128)(2,1)S(1)} %all_to_all.10.grads, ...), custom_call_target="tpu_custom_call" | custom-call | tf_op jit(solution)/shard_map/pallas_call | solution.py:439
  28.3 0.2 collective-permute-start.4
  28.5 1.0 %collective-permute-start.5 = (bf16[16,128]{1,0:T(8,128)(2,1)S(1)}, bf16[16,128]{1,0:T(8,128)(2,1)S(1)}, u32[]{:S(2)}, u32[]{:S(2)}) collective-permute-start(bf16[16,128]{1,0:T(8,128)(2,1)S(1)} %get-tuple-element.18), channel_id=1, source_target_pairs={{0,8},{4,12},{8,0},{12,4},{1,9},{5,13},{9,1},{13,5},{2,10},{6,14},... | collective-permute-start | bytes 12296 | tf_op jit(solution)/shard_map/ppermute | solution.py:469
  29.5 3.3 %collective-permute-start.6 = (bf16[16,128]{1,0:T(8,128)(2,1)S(1)}, bf16[16,128]{1,0:T(8,128)(2,1)S(1)}, u32[]{:S(2)}, u32[]{:S(2)}) collective-permute-start(bf16[16,128]{1,0:T(8,128)(2,1)S(1)} %get-tuple-element.19), channel_id=1, source_target_pairs={{0,12},{4,8},{8,4},{12,0},{1,13},{5,9},{9,5},{13,1},{2,14},{6,10},... | collective-permute-start | bytes 12296 | tf_op jit(solution)/shard_map/ppermute | solution.py:469
  32.7 0.2 collective-permute-done.5.refs_2_
  33.0 1.9 %collective-permute-done.6.refs_3_ = bf16[16,128]{1,0:T(8,128)(2,1)S(1)} collective-permute-done((bf16[16,128]{1,0:T(8,128)(2,1)S(1)}, bf16[16,128]{1,0:T(8,128)(2,1)S(1)}, u32[]{:S(2)}, u32[]{:S(2)}) %collective-permute-start.6) | collective-permute-done | bytes 4128 | tf_op jit(solution)/shard_map/ppermute | solution.py:469
  34.9 1.7 %shard_map.185 = bf16[16,16,128]{2,1,0:T(8,128)(2,1)S(1)} custom-call(f32[1]{0:T(128)S(6)} %copy.21.dose, bf16[16,128]{1,0:T(8,128)(2,1)S(1)} %get-tuple-element.16.refs_0_, bf16[16,128]{1,0:T(8,128)(2,1)S(1)} %collective-permute-done.4.refs_1_, bf16[16,128]{1,0:T(8,128)(2,1)S(1)} %collective-permute-done.5.refs_2_, ...), custom_call_target="tpu_custom_call" | custom-call | tf_op jit(solution)/shard_map/pallas_call | solution.py:439
  36.6 11.3 %all_to_all.11.grads = bf16[16,16,128]{2,1,0:T(8,128)(2,1)S(1)} all-to-all(bf16[16,16,128]{2,1,0:T(8,128)(2,1)S(1)} %shard_map.185), channel_id=1, replica_groups=mesh['groups'=2,'cells'=4,'corners'=2,'kern'=2] {'cells','corners','kern'}, dimensions={0} | all-to-all | bytes 131072 | tf_op jit(solution)/shard_map/all_to_all | solution.py:545
  47.9 1.3 %shard_map.186 = f32[8,32,128]{2,1,0:T(8,128)} custom-call(f32[8,128,128]{2,1,0:T(8,128)S(1)} %get-tuple-element.15.theta, bf16[16,16,128]{2,1,0:T(8,128)(2,1)S(1)} %all_to_all.11.grads, f32[8,8,256]{2,1,0:T(8,128)S(1)} %get-tuple-element.20.sums, bf16[128,256]{1,0:T(8,128)(2,1)S(1)} %copy-done.3, bf16[128,48]{1,0:T(8,128)(2,1)S(1)} %copy-done.9), custom_call_target="tpu_custom_call" | custom-call | tf_op jit(solution)/shard_map/pallas_call | solution.py:439
  (19 shorter events, 0.0 us)
Async XLA Ops:
  1.4 12.1 %collective-permute-start.3 = (bf16[12,40,128]{2,1,0:T(8,128)(2,1)S(1)}, bf16[12,40,128]{2,1,0:T(8,128)(2,1)S(1)}, u32[]{:S(2)}, u32[]{:S(2)}) collective-permute-start(bf16[12,40,128]{2,1,0:T(8,128)(2,1)S(1)} %shard_map.182.refs_5_.refs_4_), channel_id=1, source_target_pairs={{0,1},{1,0},{2,3},{3,2},{4,5},{5,4},{6,7},{7,6},{8,9},{9,8},{10,11... | collective-permute-start | bytes 368648 | tf_op jit(solution)/shard_map/ppermute | solution.py:469
  2.0 11.5 %copy-start.1 = (bf16[256,256]{1,0:T(8,128)(2,1)S(1)}, bf16[256,256]{1,0:T(8,128)(2,1)}, u32[]{:S(2)}) copy-start(bf16[256,256]{1,0:T(8,128)(2,1)} %constant.28.clone.refs_9_.refs_8_) | copy-start | bytes 393220
  2.0 11.5 %copy-start.2 = (bf16[256,256]{1,0:T(8,128)(2,1)S(1)}, bf16[256,256]{1,0:T(8,128)(2,1)}, u32[]{:S(2)}) copy-start(bf16[256,256]{1,0:T(8,128)(2,1)} %constant.27.clone.refs_8_.refs_7_) | copy-start | bytes 393220
  2.0 11.5 %copy-start.5 = (bf16[2,128,128]{2,1,0:T(8,128)(2,1)S(1)}, bf16[2,128,128]{2,1,0:T(8,128)(2,1)}, u32[]{:S(2)}) copy-start(bf16[2,128,128]{2,1,0:T(8,128)(2,1)} %refs_6_.1) | copy-start | bytes 196612
  2.0 11.5 %copy-start.6 = (bf16[128,224]{1,0:T(8,128)(2,1)S(1)}, bf16[128,224]{1,0:T(8,128)(2,1)}, u32[]{:S(2)}) copy-start(bf16[128,224]{1,0:T(8,128)(2,1)} %constant.31.clone.refs_12_.refs_11_) | copy-start | bytes 172036
  2.0 11.5 %copy-start.7 = (bf16[80,144]{1,0:T(8,128)(2,1)S(1)}, bf16[80,144]{1,0:T(8,128)(2,1)}, u32[]{:S(2)}) copy-start(bf16[80,144]{1,0:T(8,128)(2,1)} %constant.30.clone.refs_11_.refs_10_) | copy-start | bytes 69124
  2.0 11.5 %copy-start.8 = (bf16[144,80]{1,0:T(8,128)(2,1)S(1)}, bf16[144,80]{1,0:T(8,128)(2,1)}, u32[]{:S(2)}) copy-start(bf16[144,80]{1,0:T(8,128)(2,1)} %constant.29.clone.refs_10_.refs_9_) | copy-start | bytes 69124
  2.0 11.5 %copy-start.11 = (f32[128,256]{1,0:T(8,128)S(1)}, f32[128,256]{1,0:T(8,128)}, u32[]{:S(2)}) copy-start(f32[128,256]{1,0:T(8,128)} %constant.26.clone.refs_4_) | copy-start | bytes 393220
  2.0 11.5 %copy-start.13 = (bf16[72,128]{1,0:T(8,128)(2,1)S(1)}, bf16[72,128]{1,0:T(8,128)(2,1)}, u32[]{:S(2)}) copy-start(bf16[72,128]{1,0:T(8,128)(2,1)} %constant.32.clone.refs_13_.refs_12_) | copy-start | bytes 55300
  3.9 6.9 %collective-permute-start.2 = (bf16[144,128]{1,0:T(8,128)(2,1)S(1)}, bf16[144,128]{1,0:T(8,128)(2,1)S(1)}, u32[]{:S(2)}, u32[]{:S(2)}) collective-permute-start(bf16[144,128]{1,0:T(8,128)(2,1)S(1)} %get-tuple-element.14.refs_0_), channel_id=1, source_target_pairs={{0,12},{4,8},{8,4},{12,0},{1,13},{5,9},{9,5},{13,1},{2,14},{6,10},... | collective-permute-start | bytes 110600 | tf_op jit(solution)/shard_map/ppermute | solution.py:469
  8.6 4.9 %collective-permute-start.1 = (bf16[144,128]{1,0:T(8,128)(2,1)S(1)}, bf16[144,128]{1,0:T(8,128)(2,1)S(1)}, u32[]{:S(2)}, u32[]{:S(2)}) collective-permute-start(bf16[144,128]{1,0:T(8,128)(2,1)S(1)} %get-tuple-element.14.refs_0_), channel_id=1, source_target_pairs={{0,8},{4,12},{8,0},{12,4},{1,9},{5,13},{9,1},{13,5},{2,10},{6,14},... | collective-permute-start | bytes 110600 | tf_op jit(solution)/shard_map/ppermute | solution.py:469
  8.6 4.9 %collective-permute-start = (bf16[144,128]{1,0:T(8,128)(2,1)S(1)}, bf16[144,128]{1,0:T(8,128)(2,1)S(1)}, u32[]{:S(2)}, u32[]{:S(2)}) collective-permute-start(bf16[144,128]{1,0:T(8,128)(2,1)S(1)} %get-tuple-element.14.refs_0_), channel_id=1, source_target_pairs={{0,4},{4,0},{8,12},{12,8},{1,5},{5,1},{9,13},{13,9},{2,6},{6,2},{1... | collective-permute-start | bytes 110600 | tf_op jit(solution)/shard_map/ppermute | solution.py:469
  13.6 13.1 %copy-start = (f32[8,128,128]{2,1,0:T(8,128)S(1)}, f32[8,128,128]{2,1,0:T(8,128)}, u32[]{:S(2)}) copy-start(f32[8,128,128]{2,1,0:T(8,128)} %theta.3) | copy-start | bytes 1572868
  13.6 13.1 %copy-start.9 = (bf16[128,48]{1,0:T(8,128)(2,1)S(1)}, bf16[128,48]{1,0:T(8,128)(2,1)}, u32[]{:S(2)}) copy-start(bf16[128,48]{1,0:T(8,128)(2,1)} %constant.35.clone.ex) | copy-start | bytes 36868
  13.6 13.1 %copy-start.10 = (bf16[128,512]{1,0:T(8,128)(2,1)S(1)}, bf16[128,512]{1,0:T(8,128)(2,1)}, u32[]{:S(2)}) copy-start(bf16[128,512]{1,0:T(8,128)(2,1)} %constant.33.clone.ph) | copy-start | bytes 393220
  13.6 13.1 %copy-start.12 = (bf16[96,128]{1,0:T(8,128)(2,1)S(1)}, bf16[96,128]{1,0:T(8,128)(2,1)}, u32[]{:S(2)}) copy-start(bf16[96,128]{1,0:T(8,128)(2,1)} %constant.25.clone.fx) | copy-start | bytes 73732
  15.5 11.2 %copy-start.3 = (bf16[128,256]{1,0:T(8,128)(2,1)S(1)}, bf16[128,256]{1,0:T(8,128)(2,1)}, u32[]{:S(2)}) copy-start(bf16[128,256]{1,0:T(8,128)(2,1)} %constant.34.clone.gy) | copy-start | bytes 196612
  15.5 11.2 %copy-start.4 = (bf16[128,256]{1,0:T(8,128)(2,1)S(1)}, bf16[128,256]{1,0:T(8,128)(2,1)}, u32[]{:S(2)}) copy-start(bf16[128,256]{1,0:T(8,128)(2,1)} %constant.24.clone.fy) | copy-start | bytes 196612
  28.3 4.4 %collective-permute-start.4 = (bf16[16,128]{1,0:T(8,128)(2,1)S(1)}, bf16[16,128]{1,0:T(8,128)(2,1)S(1)}, u32[]{:S(2)}, u32[]{:S(2)}) collective-permute-start(bf16[16,128]{1,0:T(8,128)(2,1)S(1)} %get-tuple-element.17), channel_id=1, source_target_pairs={{0,4},{4,0},{8,12},{12,8},{1,5},{5,1},{9,13},{13,9},{2,6},{6,2},{1... | collective-permute-start | bytes 12296 | tf_op jit(solution)/shard_map/ppermute | solution.py:469
  28.5 4.5 %collective-permute-start.5 = (bf16[16,128]{1,0:T(8,128)(2,1)S(1)}, bf16[16,128]{1,0:T(8,128)(2,1)S(1)}, u32[]{:S(2)}, u32[]{:S(2)}) collective-permute-start(bf16[16,128]{1,0:T(8,128)(2,1)S(1)} %get-tuple-element.18), channel_id=1, source_target_pairs={{0,8},{4,12},{8,0},{12,4},{1,9},{5,13},{9,1},{13,5},{2,10},{6,14},... | collective-permute-start | bytes 12296 | tf_op jit(solution)/shard_map/ppermute | solution.py:469
  29.5 5.4 %collective-permute-start.6 = (bf16[16,128]{1,0:T(8,128)(2,1)S(1)}, bf16[16,128]{1,0:T(8,128)(2,1)S(1)}, u32[]{:S(2)}, u32[]{:S(2)}) collective-permute-start(bf16[16,128]{1,0:T(8,128)(2,1)S(1)} %get-tuple-element.19), channel_id=1, source_target_pairs={{0,12},{4,8},{8,4},{12,0},{1,13},{5,9},{9,5},{13,1},{2,14},{6,10},... | collective-permute-start | bytes 12296 | tf_op jit(solution)/shard_map/ppermute | solution.py:469
